TPU v7x, 32 devices: a whole 2x2x4 slice. The times are simulated.
32 devices in a mesh: tensor: 4 (over z), dp: 4 (over y, x), replica: 2 (over core).
Axes of the slice: x: 2, y: 2, z: 4, core: 2. Of those that a mesh axis runs over, the one named last changes fastest.
Arguments:
- states: bfloat16 [8, 256, 4096], P(('dp', 'replica')), may hold values from -6 to 6
- norm_gain: float32 [4096], replicated, may hold values from 0.26 to 4.4
- gate_up: bfloat16 [4096, 2, 14336], P('replica', None, 'tensor'), may hold values from -0.09375 to 0.09375
- cotangent: bfloat16 [8, 256, 14336], P(('dp', 'replica'), None, 'tensor'), may hold values from -120 to 120
- prompt: bfloat16 [32, 4096], replicated, may hold values from -6 to 6
- step_sizes: float32 [3], replicated, may hold values from 0.3 to 1
- insert_at: int32 [8], P(('dp', 'replica')), may hold values from 0 to 224, as said below
- lengths: int32 [8], P(('dp', 'replica')), may hold values from 128 to 256, as said below
Outputs:
- prompt_final: float32 [32, 4096], P(None, 'tensor')
- weight_step: bfloat16 [4096, 2, 14336], P(('dp', 'replica'), None, 'tensor')
Inputs may be any that keep to these rules, and one draw needn't show every extreme that they name: Each prompt lies inside its sequence: insert_at[b] + 32 <= lengths[b]; in every draw some prompt begins at row 0 and some prompt ends at the last row 255. `lengths`: in every draw some sequence has all 256 rows live and some has 128.
All inputs are finite; a program needn't handle non-finite values.
Results may differ from a plain program's by a relative error of at most 0.012.
Values may be sent and summed in bfloat16 or wider, within the bound.
A program may use at most 320 MiB of HBM per device.

v0:
```python
import jax
import jax.numpy as jnp
from jax import lax
from jax.sharding import PartitionSpec as P

D = 4096
FF = 14336


def row_scale(feature_rows):
    return lax.rsqrt(jnp.mean(feature_rows * feature_rows, axis=-1, keepdims=True) + 1e-05)


def silu_parts(gate_values):
    sigmoid_value = jax.nn.sigmoid(gate_values)
    return (
        gate_values * sigmoid_value,
        sigmoid_value * (1.0 + gate_values * (1.0 - sigmoid_value)),
    )


def hidden_grads(normalized, weight_pair, cotan_rows):
    unit_count = weight_pair.shape[1] // 2
    projected = jnp.dot(normalized, weight_pair, preferred_element_type=jnp.float32)
    activated, derivative = silu_parts(projected[:, :unit_count])
    up_part = projected[:, unit_count:]
    return jnp.concatenate(
        [cotan_rows * up_part * derivative, cotan_rows * activated], axis=1
    ).astype(jnp.bfloat16)


def norm_back(shifted, inverse_rms, norm_gain, feature_grad):
    feature_mean = jnp.mean(shifted * norm_gain * feature_grad, axis=-1, keepdims=True)
    return (
        inverse_rms * norm_gain * feature_grad
        - shifted * (inverse_rms * inverse_rms * inverse_rms) * feature_mean
    )


def per_device(states, norm_gain, gate_up, cotangent, prompt, step_sizes, insert_at, lengths):
    gathered = lax.all_gather(gate_up, "replica", axis=0, tiled=True)
    feature_count = gathered.shape[0]
    unit_count = gathered.shape[2]
    weight_pair = gathered.reshape(feature_count, 2 * unit_count)
    seq_states = states[0]
    seq_cotan = cotangent[0].astype(jnp.float32)
    prompt_start = insert_at[0]
    seq_length = lengths[0]
    prompt_count = prompt.shape[0]
    prompt_base = lax.dynamic_slice_in_dim(seq_states, prompt_start, prompt_count, 0).astype(
        jnp.float32
    )
    prompt_cotan = lax.dynamic_slice_in_dim(seq_cotan, prompt_start, prompt_count, 0)
    adversary = prompt.astype(jnp.float32)
    for attack_step in range(step_sizes.shape[0]):
        shifted = prompt_base + adversary
        inverse_rms = row_scale(shifted)
        normalized = (shifted * inverse_rms * norm_gain).astype(jnp.bfloat16)
        unit_grads = hidden_grads(normalized, weight_pair, prompt_cotan)
        feature_grad = lax.dot_general(
            unit_grads, weight_pair, (((1,), (1,)), ((), ())), preferred_element_type=jnp.float32
        )
        feature_grad = lax.psum(feature_grad, "tensor")
        summed_grad = lax.psum(
            norm_back(shifted, inverse_rms, norm_gain, feature_grad), ("dp", "replica")
        )
        adversary = adversary + step_sizes[attack_step] * summed_grad * lax.rsqrt(
            jnp.mean(summed_grad * summed_grad, axis=-1, keepdims=True) + 1e-06
        )
    full_rows = lax.dynamic_update_slice_in_dim(
        seq_states.astype(jnp.float32), prompt_base + adversary, prompt_start, 0
    )
    full_normed = (full_rows * row_scale(full_rows) * norm_gain).astype(jnp.bfloat16)
    positions = lax.broadcasted_iota(jnp.int32, (full_rows.shape[0], 1), 0)
    live_cotan = jnp.where(positions < seq_length, seq_cotan, 0.0)
    token_grads = hidden_grads(full_normed, weight_pair, live_cotan)
    received = lax.all_to_all(
        full_normed, ("dp", "replica"), split_axis=1, concat_axis=0, tiled=True
    )
    weight_grad = lax.dot_general(
        received,
        lax.all_gather(token_grads, ("dp", "replica"), axis=0, tiled=True),
        (((0,), (0,)), ((), ())),
        preferred_element_type=jnp.float32,
    )
    squares = lax.psum(jnp.sum(weight_grad * weight_grad), ("tensor", "dp", "replica"))
    weight_step = (weight_grad * lax.rsqrt(squares / (2 * D * FF) + 1e-06)).astype(jnp.bfloat16)
    weight_step = weight_step.reshape(weight_grad.shape[0], 2, unit_count)
    column_count = adversary.shape[1] // lax.axis_size("tensor")
    prompt_final = lax.dynamic_slice_in_dim(
        adversary, lax.axis_index("tensor") * column_count, column_count, 1
    )
    return (prompt_final, weight_step)


def solution(mesh):
    return jax.shard_map(
        per_device,
        mesh=mesh,
        in_specs=(
            P(("dp", "replica"), None, None),
            P(),
            P("replica", None, "tensor"),
            P(("dp", "replica"), None, "tensor"),
            P(),
            P(),
            P(("dp", "replica")),
            P(("dp", "replica")),
        ),
        out_specs=(P(None, "tensor"), P(("dp", "replica"), None, "tensor")),
        check_vma=False,
    )
```

profile of v0, /device:TPU:0, one launch (start us, length us, event | category | flops | bytes accessed | tf_op | source)
XLA Modules:
  0.0 888.1 jit_solution(5123396470353676943)
XLA Ops:
  7.2 0.7 all-gather.3.cloned.1.call-update
  8.8 3.8 convert_element_type.43
  12.8 83.6 %all-gather.3.cloned.1.call-done = bf16[4096,2,3584]{2,1,0:T(2,128)(2,1)} async-done(((bf16[2048,2,3584]{2,1,0:T(2,128)(2,1)}), bf16[4096,2,3584]{2,1,0:T(2,128)(2,1)}) %all-gather.3.cloned.1.call-update) | async-done | bytes 58720272 | tf_op jit(solution)/shard_map/all_gather | solution.py:41
  96.4 39.3 %copy.16 = bf16[512,8,2,3584]{3,1,2,0:T(8,128)(2,1)} copy(bf16[512,8,2,3584]{3,2,1,0:T(2,128)(2,1)} %bitcast.75) | data formatting | bytes 117440512
  135.7 21.5 %fusion.23 = f32[32,7168]{1,0:T(8,128)S(1)} fusion(bf16[4096,7168]{1,0:T(8,128)(2,1)} %bitcast.68, bf16[32,4096]{1,0:T(8,128)(2,1)S(1)} %copy-done.2, f32[4096]{0:T(1024)S(1)} %copy-done.5, f32[32]{0:T(128)S(1)} %get-tuple-element.24, bf16[1,256,4096]{2,1,0:T(8,128)(2,1)S(1)} %copy-done.1, s32[]{:T(128)S(6)} %select_n.12), kind=kOutput, calls=%fused_computation.64 | convolution fusion | flops 1879834624 | bytes 60178948 | tf_op jit(solution)/shard_map/dot_general | solution.py:24
  157.2 1.3 fusion.7
  158.5 24.7 %fusion.8 = f32[32,4096]{1,0:T(8,128)} fusion(bf16[4096,7168]{1,0:T(8,128)(2,1)} %bitcast.69, bf16[32,3584]{1,0:T(8,128)(2,1)S(1)} %get-tuple-element.15, bf16[32,3584]{1,0:T(8,128)(2,1)S(1)} %get-tuple-element.14), kind=kOutput, calls=%fused_computation.43 | convolution fusion | flops 1879965696 | bytes 59703296 | tf_op jit(solution)/shard_map/dot_general | solution.py:60
  183.3 39.6 %all-reduce.7.cloned.1.call-done = f32[32,4096]{1,0:T(8,128)} async-done(((f32[32,4096]{1,0:T(8,128)}), f32[32,4096]{1,0:T(8,128)}) %all-reduce.7.cloned.1.call-update) | async-done | bytes 524304 | tf_op jit(solution)/shard_map/psum | solution.py:63
  222.9 1.3 multiply_reduce_fusion.9
  224.2 2.0 multiply_subtract_fusion.2
  226.9 54.0 %all-reduce.9.cloned.1.call-done = f32[32,4096]{1,0:T(8,128)} async-done(((f32[32,4096]{1,0:T(8,128)}), f32[32,4096]{1,0:T(8,128)}) %all-reduce.9.cloned.1.call-update) | async-done | bytes 524304 | tf_op jit(solution)/shard_map/psum | solution.py:64
  280.9 1.2 multiply_reduce_fusion.8
  282.1 1.9 multiply_reduce_fusion.7
  284.1 21.5 %fusion.24 = f32[32,7168]{1,0:T(8,128)S(1)} fusion(bf16[4096,7168]{1,0:T(8,128)(2,1)} %bitcast.70, f32[32,4096]{1,0:T(8,128)S(1)} %get-tuple-element.7, f32[32]{0:T(128)S(1)} %get-tuple-element.22, f32[4096]{0:T(1024)S(1)} %copy-done.5), kind=kOutput, calls=%fused_computation.65 | convolution fusion | flops 1879441408 | bytes 60178560 | tf_op jit(solution)/shard_map/dot_general | solution.py:24
  305.6 1.3 fusion.5
  306.9 24.7 %fusion.12 = f32[32,4096]{1,0:T(8,128)} fusion(bf16[4096,7168]{1,0:T(8,128)(2,1)} %bitcast.71, bf16[32,3584]{1,0:T(8,128)(2,1)S(1)} %get-tuple-element.13, bf16[32,3584]{1,0:T(8,128)(2,1)S(1)} %get-tuple-element.12), kind=kOutput, calls=%fused_computation.47 | convolution fusion | flops 1879965696 | bytes 59703296 | tf_op jit(solution)/shard_map/dot_general | solution.py:60
  331.7 37.7 %all-reduce.11.cloned.1.call-done = f32[32,4096]{1,0:T(8,128)} async-done(((f32[32,4096]{1,0:T(8,128)}), f32[32,4096]{1,0:T(8,128)}) %all-reduce.11.cloned.1.call-update) | async-done | bytes 524304 | tf_op jit(solution)/shard_map/psum | solution.py:63
  369.3 1.2 multiply_reduce_fusion.6
  370.6 2.0 multiply_subtract_fusion.1
  373.2 54.1 %all-reduce.13.cloned.1.call-done = f32[32,4096]{1,0:T(8,128)} async-done(((f32[32,4096]{1,0:T(8,128)}), f32[32,4096]{1,0:T(8,128)}) %all-reduce.13.cloned.1.call-update) | async-done | bytes 524304 | tf_op jit(solution)/shard_map/psum | solution.py:64
  427.3 1.2 multiply_reduce_fusion.5
  428.5 2.6 multiply_reduce_fusion.4
  431.1 21.4 %fusion.25 = f32[32,7168]{1,0:T(8,128)S(1)} fusion(bf16[4096,7168]{1,0:T(8,128)(2,1)} %bitcast.72, f32[32]{0:T(128)S(1)} %get-tuple-element.20, f32[4096]{0:T(1024)S(1)} %copy-done.5, f32[32,4096]{1,0:T(8,128)S(1)} %get-tuple-element.5, bf16[1,256,4096]{2,1,0:T(8,128)(2,1)S(1)} %copy-done.1, s32[]{:T(128)S(6)} %select_n.12), kind=kOutput, calls=%fused_computation.66 | convolution fusion | flops 1879703552 | bytes 60441092 | tf_op jit(solution)/shard_map/dot_general | solution.py:24
  452.5 1.3 fusion.3
  453.9 24.7 %fusion.16 = f32[32,4096]{1,0:T(8,128)} fusion(bf16[4096,7168]{1,0:T(8,128)(2,1)} %bitcast.73, bf16[32,3584]{1,0:T(8,128)(2,1)S(1)} %get-tuple-element.11, bf16[32,3584]{1,0:T(8,128)(2,1)S(1)} %get-tuple-element.10), kind=kOutput, calls=%fused_computation.51 | convolution fusion | flops 1879965696 | bytes 59703296 | tf_op jit(solution)/shard_map/dot_general | solution.py:60
  478.6 2.5 copy.13
  481.2 35.2 %all-reduce.15.cloned.1.call-done = f32[32,4096]{1,0:T(8,128)} async-done(((f32[32,4096]{1,0:T(8,128)}), f32[32,4096]{1,0:T(8,128)}) %all-reduce.15.cloned.1.call-update) | async-done | bytes 524304 | tf_op jit(solution)/shard_map/psum | solution.py:63
  516.3 1.3 multiply_reduce_fusion.3
  517.6 2.0 multiply_subtract_fusion
  519.9 3.9 bitcast_convert_fusion
  524.5 49.9 %all-reduce.17.cloned.1.call-done = f32[32,4096]{1,0:T(8,128)} async-done(((f32[32,4096]{1,0:T(8,128)}), f32[32,4096]{1,0:T(8,128)}) %all-reduce.17.cloned.1.call-update) | async-done | bytes 524304 | tf_op jit(solution)/shard_map/psum | solution.py:64
  574.4 1.2 multiply_reduce_fusion.2
  575.5 2.7 convert_add_fusion
  578.8 10.4 %dynamic_update_slice.3 = f32[256,4096]{0,1:T(8,128)} dynamic-update-slice(f32[256,4096]{0,1:T(8,128)} %bitcast_convert_fusion, f32[32,4096]{0,1:T(8,128)S(1)} %copy.14, s32[]{:T(128)S(6)} %select_n.12, s32[]{:T(128)} %constant.15.clone.1) | dynamic-update-slice | bytes 1048580 | tf_op jit(solution)/shard_map/dynamic_update_slice | solution.py:70
  589.2 2.9 multiply_reduce_fusion.1
  592.7 1.7 multiply_convert_fusion.1
  594.4 28.3 %fusion.39 = f32[256,7168]{1,0:T(8,128)} fusion(bf16[256,4096]{0,1:T(8,128)(2,1)} %multiply_convert_fusion.1, bf16[4096,7168]{1,0:T(8,128)(2,1)} %bitcast.74), kind=kOutput, calls=%fused_computation.95 | convolution fusion | flops 15032385536 | bytes 68157440 | tf_op jit(solution)/shard_map/dot_general | solution.py:24
  622.8 4.1 fusion.1
  626.9 2.3 pad_maximum_fusion
  629.2 3.8 all-to-all-start
  633.0 1.6 constant_dynamic-slice_fusion
  634.6 40.3 %all-to-all-done = bf16[256,8,512]{0,2,1:T(8,128)(2,1)S(1)} async-done(((bf16[256,8,512]{0,2,1:T(8,128)(2,1)}), bf16[256,8,512]{0,2,1:T(8,128)(2,1)S(1)}, u32[]{:S(2)}, u32[]{:S(2)}) %all-to-all-start) | async-done | bytes 2097184 | tf_op jit(solution)/shard_map/all_to_all | solution.py:77
  674.9 2.4 copy.15
  677.3 110.5 %all-gather.5.cloned.1.call-done = bf16[2048,7168]{1,0:T(8,128)(2,1)} async-done(((bf16[256,7168]{1,0:T(8,128)(2,1)}), bf16[2048,7168]{1,0:T(8,128)(2,1)}) %all-gather.5.cloned.1.call-update) | async-done | bytes 29360144 | tf_op jit(solution)/shard_map/all_gather | solution.py:82
  787.7 26.1 %multiply_reduce_fusion = (f32[]{:T(128)}, f32[512,7168]{1,0:T(8,128)}) fusion(bf16[2048,512]{1,0:T(8,128)(2,1)} %bitcast.77, bf16[2048,7168]{1,0:T(8,128)(2,1)} %all-gather.5.cloned.1.call-done), kind=kOutput, calls=%fused_computation.1 | convolution fusion | flops 15039725568 | bytes 46137348 | tf_op jit(solution)/shard_map/dot_general | solution.py:80
  813.9 39.8 %psum.55 = f32[]{:T(128)} all-reduce(f32[]{:T(128)} %get-tuple-element.25), channel_id=1, replica_groups=mesh['tensor'=4,'dp'=4,'replica'=2] {'tensor','dp','replica'}, use_global_device_ids=true, to_apply=%region_17.18 | all-reduce | flops 1 | bytes 8 | tf_op jit(solution)/shard_map/psum | solution.py:86
  854.3 9.8 %multiply_convert_fusion = bf16[512,7168]{1,0:T(8,128)(2,1)} fusion(f32[512,7168]{1,0:T(8,128)} %get-tuple-element.26, f32[]{:T(128)S(6)} %rsqrt.75), kind=kLoop, calls=%fused_computation | loop fusion | flops 7340032 | bytes 22020100 | tf_op jit(solution)/shard_map/convert_element_type | solution.py:87
  864.1 16.9 %reshape.113 = bf16[512,2,3584]{2,1,0:T(2,128)(2,1)} reshape(bf16[512,7168]{1,0:T(8,128)(2,1)} %multiply_convert_fusion) | data formatting | bytes 14680064 | tf_op jit(solution)/shard_map/reshape | solution.py:88
  (43 shorter events, 3.2 us)
Async XLA Ops:
  7.2 89.3 %all-gather.3.cloned.1.call-start = ((), (), s32[]{:S(2)}) async-start(), calls=%async_computation.1 | async-start | bytes 88080384 | tf_op jit(solution)/shard_map/all_gather | solution.py:41
  7.9 4.6 copy-start.1
  7.9 4.6 copy-start.2
  7.9 215.0 %all-reduce.7.cloned.1.call-start = ((), (), s32[]{:S(2)}) async-start(), calls=%async_computation.2 | async-start | bytes 1048576 | tf_op jit(solution)/shard_map/psum | solution.py:63
  96.4 39.3 %copy-start.5 = (f32[4096]{0:T(1024)S(1)}, f32[4096]{0:T(1024)}, u32[]{:S(2)}) copy-start(f32[4096]{0:T(1024)} %param.9) | copy-start | bytes 49156
  183.2 43.1 %copy-start.6 = (f32[3]{0:T(128)S(1)}, f32[3]{0:T(128)}, u32[]{:S(2)}) copy-start(f32[3]{0:T(128)} %param.13) | copy-start | bytes 40
  183.2 97.7 %all-reduce.9.cloned.1.call-start = ((), (), s32[]{:S(2)}) async-start(), calls=%async_computation.3 | async-start | bytes 1048576 | tf_op jit(solution)/shard_map/psum | solution.py:64
  226.2 143.1 %all-reduce.11.cloned.1.call-start = ((), (), s32[]{:S(2)}) async-start(), calls=%async_computation.4 | async-start | bytes 1048576 | tf_op jit(solution)/shard_map/psum | solution.py:63
  331.6 96.9 %copy-start.4 = (f32[32,4096]{1,0:T(8,128)S(1)}, f32[32,4096]{1,0:T(8,128)}, u32[]{:S(2)}) copy-start(f32[32,4096]{1,0:T(8,128)} %all-reduce.9.cloned.1.call-done) | copy-start | bytes 1572868
  331.6 95.7 %all-reduce.13.cloned.1.call-start = ((), (), s32[]{:S(2)}) async-start(), calls=%async_computation.5 | async-start | bytes 1048576 | tf_op jit(solution)/shard_map/psum | solution.py:64
  372.6 143.8 %all-reduce.15.cloned.1.call-start = ((), (), s32[]{:S(2)}) async-start(), calls=%async_computation.6 | async-start | bytes 1048576 | tf_op jit(solution)/shard_map/psum | solution.py:63
  478.6 95.8 %all-reduce.17.cloned.1.call-start = ((), (), s32[]{:S(2)}) async-start(), calls=%async_computation.7 | async-start | bytes 1048576 | tf_op jit(solution)/shard_map/psum | solution.py:64
  519.7 268.1 %all-gather.5.cloned.1.call-start = ((), (), s32[]{:S(2)}) async-start(), calls=%async_computation.8 | async-start | bytes 33030144 | tf_op jit(solution)/shard_map/all_gather | solution.py:82
  589.2 3.4 copy-start
  594.4 28.3 %copy-start.3 = (bf16[1,256,3584]{2,1,0:T(8,128)(2,1)S(1)}, bf16[1,256,3584]{2,1,0:T(8,128)(2,1)}, u32[]{:S(2)}) copy-start(bf16[1,256,3584]{2,1,0:T(8,128)(2,1)} %param.11) | copy-start | bytes 5505028
  629.2 45.7 %all-to-all-start = ((bf16[256,8,512]{0,2,1:T(8,128)(2,1)}), bf16[256,8,512]{0,2,1:T(8,128)(2,1)S(1)}, u32[]{:S(2)}, u32[]{:S(2)}) async-start(bf16[256,8,512]{0,2,1:T(8,128)(2,1)} %bitcast.8), calls=%async_computation | async-start | bytes 4194304 | tf_op jit(solution)/shard_map/all_to_all | solution.py:77
Sparse Core Ops, SparseCore 0:
  9.5 86.8 all-gather.2
  183.4 39.4 all-reduce.6
  226.4 54.5 all-reduce.8
  331.7 37.5 all-reduce.10
  372.7 54.5 all-reduce.12
  478.7 37.5 all-reduce.14
  519.8 54.5 all-reduce.16
  629.3 158.4 all-gather.4
where the time goes:
time: 899 us; the launch traced here: 888 us
  waiting for transfers between devices  506 us (56%)
  matrix products  193 us (21%)
  local copies, waits for them, and re-layouts  74.8 us (8%)
  other arithmetic  53.3 us (6%)
  blocking collectives  39.8 us (4%)
  between operations  16.7 us (2%)
    psum x3, waiting for transfers between devices, per_device(): lax.psum(norm_back(shifted, inverse_rms, norm_gain, feature_grad), ('dp',...  158 us
    psum x3, waiting for transfers between devices, per_device(): feature_grad = lax.psum(feature_grad, 'tensor')  112 us
    all_gather x1, waiting for transfers between devices, per_device(): lax.all_gather(token_grads, ('dp', 'replica'), axis=0, tiled=True)  110 us
    dot_general x4, matrix products, hidden_grads(): jnp.dot(normalized, weight_pair, preferred_element_type=jnp.float32)  92.8 us
    all_gather x1, waiting for transfers between devices, per_device(): gathered = lax.all_gather(gate_up, 'replica', axis=0, tiled=True)  83.6 us
    dot_general x3, matrix products, per_device(): lax.dot_general(unit_grads, weight_pair, (((1,), (1,)), ((), ())), prefer...  74.1 us
    unnamed x16, local copies, waits for them, and re-layouts  42.3 us
    all_to_all x1, waiting for transfers between devices, per_device(): lax.all_to_all(full_normed, ('dp', 'replica'), split_axis=1, concat_axis=...  40.3 us
  transfers between devices with their start and end apart: 9, of which 9 were waited for; matrix products, arithmetic and copies ran while one was open for 2% of the time, Pallas kernels for 0%

commit v1 on v0

v1 whole, which is shorter than its diff:
```python
import functools

import jax
import jax.numpy as jnp
from jax import lax
from jax.experimental import pallas as pl
from jax.experimental.pallas import tpu as pltpu
from jax.sharding import PartitionSpec as P

D = 4096
FF = 14336
MESH = pl.DeviceIdType.MESH


def row_scale(feature_rows):
    return lax.rsqrt(jnp.mean(feature_rows * feature_rows, axis=-1, keepdims=True) + 1e-05)


def silu_parts(gate_values):
    sigmoid_value = jax.nn.sigmoid(gate_values)
    return (
        gate_values * sigmoid_value,
        sigmoid_value * (1.0 + gate_values * (1.0 - sigmoid_value)),
    )


def hidden_grads(normalized, weight_pair, cotan_rows):
    unit_count = weight_pair.shape[1] // 2
    projected = jnp.dot(normalized, weight_pair, preferred_element_type=jnp.float32)
    activated, derivative = silu_parts(projected[:, :unit_count])
    up_part = projected[:, unit_count:]
    return jnp.concatenate(
        [cotan_rows * up_part * derivative, cotan_rows * activated], axis=1
    ).astype(jnp.bfloat16)


def step_kernel(
    tensors, chips, cores, partial_ref, adversary_ref, step_ref, out_ref,
    plane_buf, line_buf, mine, send1, recv1, send2, recv2, send3, recv3, send4, recv4,
):
    group = chips * cores
    t = lax.axis_index("tensor")
    g = lax.axis_index("dp") * cores + lax.axis_index("replica")
    rows = partial_ref.shape[0] // group
    own = rows // tensors
    plane = [lax.rem(g + k, group) for k in range(1, group)]
    line = [lax.rem(t + k, tensors) for k in range(1, tensors)]
    plane_ids = [{"dp": p // cores, "replica": lax.rem(p, cores)} for p in plane]
    line_ids = [{"tensor": p} for p in line]

    barrier = pltpu.get_barrier_semaphore()
    for device in plane_ids + line_ids:
        pl.semaphore_signal(barrier, inc=1, device_id=device, device_id_type=MESH)
    pl.semaphore_wait(barrier, group + tensors - 2)

    def exchange(pairs, ids, sends, recvs):
        copies = []
        for k, ((source, target), device) in enumerate(zip(pairs, ids)):
            copy = pltpu.make_async_remote_copy(
                src_ref=source, dst_ref=target, send_sem=sends.at[k], recv_sem=recvs.at[k],
                device_id=device, device_id_type=MESH,
            )
            copy.start()
            copies.append(copy)
        return copies

    first = exchange(
        [(partial_ref.at[pl.ds(p * rows, rows)], plane_buf.at[k]) for k, p in enumerate(plane)],
        plane_ids, send1, recv1,
    )
    total = partial_ref[pl.ds(g * rows, rows)]
    for k, copy in enumerate(first):
        copy.wait_recv()
        total = total + plane_buf[k]
    mine[...] = total
    second = exchange(
        [(mine.at[pl.ds(p * own, own)], line_buf.at[k]) for k, p in enumerate(line)],
        line_ids, send2, recv2,
    )
    grad = mine[pl.ds(t * own, own)]
    for k, copy in enumerate(second):
        copy.wait_recv()
        grad = grad + line_buf[k]
    square = jnp.sum(jnp.sum(grad * grad, axis=2, keepdims=True), axis=1, keepdims=True)
    count = partial_ref.shape[1] * partial_ref.shape[2]
    row = g * rows + t * own
    block = pl.ds(row, own)
    out_ref[block] = adversary_ref[block] + step_ref[0] * grad * lax.rsqrt(square / count + 1e-06)
    third = exchange([(out_ref.at[block], out_ref.at[block])] * len(line), line_ids, send3, recv3)
    for copy in third:
        copy.wait_recv()
    wide = pl.ds(g * rows, rows)
    fourth = exchange([(out_ref.at[wide], out_ref.at[wide])] * len(plane), plane_ids, send4, recv4)
    for copy in fourth:
        copy.wait_recv()
    for copy in first + second + third + fourth:
        copy.wait_send()


def apply_step(partial, adversary, step_size):
    tensors, chips, cores = (lax.axis_size(a) for a in ("tensor", "dp", "replica"))
    group = chips * cores
    count, width = partial.shape
    if count % (group * tensors) == 0 and width % 1024 == 0:
        shape = (count, 8, width // 8)
        rows = count // group
        own = rows // tensors
        dma = pltpu.SemaphoreType.DMA
        vmem = pl.BlockSpec(memory_space=pltpu.VMEM)
        result = pl.pallas_call(
            functools.partial(step_kernel, tensors, chips, cores),
            out_shape=jax.ShapeDtypeStruct(shape, jnp.float32),
            in_specs=[vmem, vmem, pl.BlockSpec(memory_space=pltpu.SMEM)],
            out_specs=vmem,
            scratch_shapes=[
                pltpu.VMEM((group - 1, rows) + shape[1:], jnp.float32),
                pltpu.VMEM((tensors - 1, own) + shape[1:], jnp.float32),
                pltpu.VMEM((rows,) + shape[1:], jnp.float32),
            ]
            + [dma((group - 1,))] * 2 + [dma((tensors - 1,))] * 4 + [dma((group - 1,))] * 2,
            compiler_params=pltpu.CompilerParams(
                collective_id=0, has_side_effects=True, vmem_limit_bytes=16 << 20
            ),
            name="attack_step",
        )(partial.reshape(shape), adversary.reshape(shape), step_size)
        return result.reshape(count, width)
    grad = lax.psum(partial, ("tensor", "dp", "replica"))
    scale = lax.rsqrt(jnp.mean(grad * grad, axis=-1, keepdims=True) + 1e-06)
    return adversary + step_size[0] * grad * scale


def norm_kernel(start_ref, state_ref, parts_ref, gain_ref, out_ref):
    slots = parts_ref.shape[0] // 3
    tokens = state_ref.shape[1]
    shape = (tokens, 3 * slots)
    slot = lax.broadcasted_iota(jnp.int32, shape, 0) - start_ref[pl.program_id(0)]
    column = lax.rem(lax.broadcasted_iota(jnp.int32, shape, 1), slots)
    placed = jnp.dot(
        jnp.where(slot == column, 1.0, 0.0).astype(jnp.bfloat16), parts_ref[...],
        preferred_element_type=jnp.float32,
    )
    rows = state_ref[0].astype(jnp.float32) + placed
    scale = lax.rsqrt(jnp.mean(rows * rows, axis=-1, keepdims=True) + 1e-05)
    out_ref[0] = (rows * scale * gain_ref[...]).astype(jnp.bfloat16)


def normed_rows(starts, states, parts, gain):
    count, tokens, width = states.shape
    return pl.pallas_call(
        norm_kernel,
        out_shape=jax.ShapeDtypeStruct(states.shape, jnp.bfloat16),
        grid_spec=pltpu.PrefetchScalarGridSpec(
            num_scalar_prefetch=1,
            grid=(count,),
            in_specs=[
                pl.BlockSpec((1, tokens, width), lambda b, s: (b, 0, 0)),
                pl.BlockSpec(parts.shape, lambda b, s: (0, 0)),
                pl.BlockSpec((1, width), lambda b, s: (0, 0)),
            ],
            out_specs=pl.BlockSpec((1, tokens, width), lambda b, s: (b, 0, 0)),
        ),
        compiler_params=pltpu.CompilerParams(vmem_limit_bytes=48 << 20),
        cost_estimate=pl.CostEstimate(
            flops=count * tokens * width * 200, bytes_accessed=count * tokens * width * 4,
            transcendentals=0,
        ),
        name="normed_rows",
    )(starts, states, parts, gain.reshape(1, width)).reshape(count * tokens, width)


def per_device(states, norm_gain, gate_up, cotangent, prompt, step_sizes, insert_at, lengths):
    chips, cores = lax.axis_size("dp"), lax.axis_size("replica")
    chip, core = lax.axis_index("dp"), lax.axis_index("replica")
    half, _, shard_units = gate_up.shape
    units = shard_units // chips
    count = prompt.shape[0]
    tokens = states.shape[1]
    width = half * cores

    unit_slice = lax.dynamic_slice_in_dim(gate_up, chip * units, units, 2)
    weight_pair = lax.all_gather(
        unit_slice.reshape(half, 2 * units), "replica", axis=0, tiled=True
    )

    seq_states, seq_cotan, prompt_start = states[0], cotangent[0], insert_at[0]
    package = jnp.concatenate(
        [
            lax.dynamic_slice_in_dim(seq_states, prompt_start, count, 0),
            lax.dynamic_slice_in_dim(seq_cotan, prompt_start, count, 0),
        ],
        axis=1,
    )
    package = lax.all_gather(package, "dp", axis=0, tiled=False)
    prompt_base = package[:, :, :width].astype(jnp.float32)
    prompt_cotan = (
        lax.dynamic_slice_in_dim(package, width + chip * units, units, 2)
        .reshape(chips * count, units)
        .astype(jnp.float32)
    )

    swap = [(i, (i + 1) % cores) for i in range(cores)]
    own_states = lax.all_gather(seq_states, "dp", axis=0, tiled=False)
    other_states = lax.ppermute(own_states, "replica", swap)
    own_starts = lax.all_gather(insert_at, "dp", axis=0, tiled=True)
    other_starts = lax.ppermute(own_starts, "replica", swap)
    positions = lax.broadcasted_iota(jnp.int32, (tokens, 1), 0)
    live_cotan = jnp.where(positions < lengths[0], seq_cotan, jnp.zeros_like(seq_cotan))

    def shifted_perm(k):
        return [(i, (i + k) % chips) for i in range(chips)]

    cotan_blocks = []
    for k in range(chips):
        block = lax.dynamic_slice_in_dim(live_cotan, lax.rem(chip + k, chips) * units, units, 1)
        cotan_blocks.append(lax.ppermute(block, "dp", shifted_perm(k)) if k else block)
    stacked = jnp.stack(cotan_blocks)
    token_cotan = jnp.concatenate(
        [
            lax.dynamic_index_in_dim(stacked, lax.rem(chip - j + chips, chips), 0, keepdims=False)
            for j in range(chips)
        ],
        axis=0,
    )

    adversary = prompt.astype(jnp.float32)
    for attack_step in range(step_sizes.shape[0]):
        shifted = prompt_base + adversary[None]
        inverse_rms = row_scale(shifted)
        normalized = (shifted * inverse_rms * norm_gain).astype(jnp.bfloat16)
        unit_grads = hidden_grads(normalized.reshape(chips * count, width), weight_pair, prompt_cotan)
        feature_grad = lax.dot_general(
            unit_grads, weight_pair, (((1,), (1,)), ((), ())), preferred_element_type=jnp.float32
        ).reshape(chips, count, width)
        scaled = norm_gain * feature_grad
        feature_mean = jnp.mean(shifted * scaled, axis=-1, keepdims=True)
        partial = jnp.sum(
            inverse_rms * scaled - shifted * (inverse_rms * inverse_rms * inverse_rms) * feature_mean,
            axis=0,
        )
        adversary = apply_step(partial, adversary, step_sizes[attack_step : attack_step + 1])

    high = lax.reduce_precision(adversary, 8, 7)
    middle = lax.reduce_precision(adversary - high, 8, 7)
    low = adversary - high - middle
    parts = jnp.concatenate([high, middle, low], axis=0).astype(jnp.bfloat16)
    own_normed = normed_rows(own_starts, own_states, parts, norm_gain)
    own_grads = hidden_grads(own_normed, weight_pair, token_cotan.astype(jnp.float32))
    other_grads = lax.ppermute(own_grads, "replica", swap)
    other_normed = normed_rows(other_starts, other_states, parts, norm_gain)

    block_width = width // (chips * cores)
    dims = (((0,), (0,)), ((), ()))
    squares = 0.0
    received = [None] * chips
    for k in [2 % chips, *[i for i in range(1, chips) if i != 2 % chips], 0] if chips > 2 else range(chips):
        start = (lax.rem(chip + k, chips) * cores + core) * block_width
        block = lax.dot_general(
            lax.dynamic_slice_in_dim(own_normed, start, block_width, 1), own_grads, dims,
            preferred_element_type=jnp.float32,
        ) + lax.dot_general(
            lax.dynamic_slice_in_dim(other_normed, start, block_width, 1), other_grads, dims,
            preferred_element_type=jnp.float32,
        )
        squares = squares + jnp.sum(block * block)
        sent = block.astype(jnp.bfloat16)
        received[k] = lax.ppermute(sent, "dp", shifted_perm(k)) if k else sent
    squares = lax.psum(squares, ("tensor", "dp", "replica"))
    scale = lax.rsqrt(squares / (2 * D * FF) + 1e-06)
    stacked = jnp.stack(received)
    pieces = [
        lax.dynamic_index_in_dim(stacked, lax.rem(chip - j + chips, chips), 0, keepdims=False)
        for j in range(chips)
    ]
    weight_step = jnp.concatenate(
        [piece.reshape(block_width, 2, units) for piece in pieces], axis=2
    )
    weight_step = (weight_step.astype(jnp.float32) * scale).astype(jnp.bfloat16)
    column_count = width // lax.axis_size("tensor")
    prompt_final = lax.dynamic_slice_in_dim(
        adversary, lax.axis_index("tensor") * column_count, column_count, 1
    )
    return (prompt_final, weight_step)


def solution(mesh):
    return jax.shard_map(
        per_device,
        mesh=mesh,
        in_specs=(
            P(("dp", "replica"), None, None),
            P(),
            P("replica", None, "tensor"),
            P(("dp", "replica"), None, "tensor"),
            P(),
            P(),
            P(("dp", "replica")),
            P(("dp", "replica")),
        ),
        out_specs=(P(None, "tensor"), P(("dp", "replica"), None, "tensor")),
        check_vma=False,
    )
```

time: 899 us -> 549 us (0.61)
  waiting for transfers between devices: 506 us -> 115 us
  Pallas kernels: 0 us -> 95.4 us
  matrix products: 193 us -> 114 us
  blocking collectives: 39.8 us -> 116 us
  local copies, waits for them, and re-layouts: 74.8 us -> 40.2 us
  other arithmetic: 53.3 us -> 36 us
    psum x6 -> x0, waiting for transfers between devices: 270 us -> none  [the longest x3 158 us: per_device(): lax.psum(norm_back(shifted, inverse_rms, norm_gain, feature_grad), ('dp',...]
    pallas_call x0 -> x5, Pallas kernels: none -> 95.4 us  [the longest x3 75 us: apply_step(): pl.pallas_call(functools.partial(step_kernel, tensors, chips, cores), out...]
    all_gather x2 -> x3, waiting for transfers between devices: 194 us -> 114 us  [the longest x1 84.8 us: per_device(): own_states = lax.all_gather(seq_states, 'dp', axis=0, tiled=False)]
    dot_general x4, matrix products: 92.8 us -> 41.2 us  [hidden_grads(): jnp.dot(normalized, weight_pair, preferred_element_type=jnp.float32)]
    psum x1, blocking collectives: 39.8 us -> 90.4 us  [per_device(): squares = lax.psum(squares, ('tensor', 'dp', 'replica'))]
    dot_general x3, matrix products: 74.1 us -> 30.2 us  [per_device(): lax.dot_general(unit_grads, weight_pair, (((1,), (1,)), ((), ())), prefer...]
    all_to_all x1 -> x0, waiting for transfers between devices: 40.3 us -> none  [per_device(): lax.all_to_all(full_normed, ('dp', 'replica'), split_axis=1, concat_axis=...]
    unnamed x16 -> x37, local copies, waits for them, and re-layouts: 42.3 us -> 9.8 us
  transfers between devices with their start and end apart: 9 -> 12, of which waited for: 9 -> 3; matrix products, arithmetic and copies ran while one was open for 2% -> 26% of each run, Pallas kernels for 0% -> 18%
where the time goes in v1:
time: 549 us; the launch traced here: 544 us
  blocking collectives  116 us (21%)
  waiting for transfers between devices  115 us (21%)
  matrix products  114 us (21%)
  Pallas kernels  95.4 us (17%)
  local copies, waits for them, and re-layouts  40.2 us (7%)
  other arithmetic  36 us (7%)
  between operations  19.2 us (3%)
  starting transfers between devices  9.03 us (2%)
    psum x1, blocking collectives, per_device(): squares = lax.psum(squares, ('tensor', 'dp', 'replica'))  90.4 us
    all_gather x1, waiting for transfers between devices, per_device(): own_states = lax.all_gather(seq_states, 'dp', axis=0, tiled=False)  84.8 us
    pallas_call x3, Pallas kernels, apply_step(): pl.pallas_call(functools.partial(step_kernel, tensors, chips, cores), out...  75 us
    dot_general x4, matrix products, hidden_grads(): jnp.dot(normalized, weight_pair, preferred_element_type=jnp.float32)  41.2 us
    dot_general x3, matrix products, per_device(): lax.dot_general(unit_grads, weight_pair, (((1,), (1,)), ((), ())), prefer...  30.2 us
    all_gather x1, waiting for transfers between devices, per_device(): lax.all_gather(unit_slice.reshape(half, 2 * units), 'replica', axis=0, ti...  29.2 us
    dot_general x4, matrix products, per_device(): lax.dot_general(lax.dynamic_slice_in_dim(other_normed, start, block_width...  25.7 us
    unnamed x1, blocking collectives  25.2 us
  transfers between devices with their start and end apart: 12, of which 3 were waited for; matrix products, arithmetic and copies ran while one was open for 26% of the time, Pallas kernels for 18%

profile of v1, /device:TPU:0, one launch (start us, length us, event | category | flops | bytes accessed | tf_op | source)
XLA Modules:
  0.0 544.4 jit_solution(8163496330888014251)
XLA Ops:
  7.9 1.0 dynamic-slice_bitcast_fusion.6
  8.9 1.0 dynamic-slice_bitcast_fusion.5
  9.9 0.9 pad_maximum_fusion.5
  11.6 6.5 %constant_dynamic-slice_fusion.8 = bf16[2048,2,896]{2,1,0:T(2,128)(2,1)S(1)} fusion(bf16[2048,2,3584]{2,1,0:T(2,128)(2,1)} %param.10, s32[]{:T(128)S(6)} %select_n.65), kind=kLoop, calls=%fused_computation.129 | loop fusion | bytes 14680068 | tf_op jit(solution)/shard_map/dynamic_slice | solution.py:180
  18.1 4.6 copy.10
  24.6 3.9 collective-permute-start.2
  30.3 0.8 dynamic-update-slice
  31.1 25.2 %all-reduce.start_ref = s32[4]{0:T(128)S(1)} all-reduce(s32[4]{0:T(128)S(1)} %dynamic-update-slice), channel_id=1, replica_groups=mesh['tensor'=4,'dp'=4,'replica'=2] {'dp'}, use_global_device_ids=true, to_apply=%add | all-reduce | flops 4 | bytes 32
  57.4 0.8 copy-done.9
  58.2 1.6 pad_maximum_fusion.2
  59.8 1.3 dynamic-slice_bitcast_fusion.3
  61.3 1.1 constant_dynamic-slice_fusion.9
  62.4 1.6 fusion.29
  64.0 1.3 fusion.31
  65.4 84.8 %all-gather.7.cloned.1.call-done.state_ref = bf16[4,256,4096]{2,1,0:T(8,128)(2,1)} async-done(((bf16[1,256,4096]{2,1,0:T(8,128)(2,1)}), bf16[4,256,4096]{2,1,0:T(8,128)(2,1)}) %all-gather.7.cloned.1.call-update) | async-done | bytes 8388624 | tf_op jit(solution)/shard_map/all_gather | solution.py:202
  150.2 29.2 %all-gather.5.cloned.1.call-done = bf16[4096,1792]{1,0:T(8,128)(2,1)} async-done(((bf16[2048,1792]{1,0:T(8,128)(2,1)}), bf16[4096,1792]{1,0:T(8,128)(2,1)}) %all-gather.5.cloned.1.call-update) | async-done | bytes 14680080 | tf_op jit(solution)/shard_map/all_gather | solution.py:181
  179.4 7.6 %fusion.84 = f32[128,1792]{1,0:T(8,128)S(1)} fusion(bf16[128,4096]{1,0:T(8,128)(2,1)} %bitcast.128, bf16[4096,1792]{1,0:T(8,128)(2,1)} %all-gather.5.cloned.1.call-done), kind=kOutput, calls=%fused_computation.145 | convolution fusion | flops 1879048192 | bytes 16646144 | tf_op jit(solution)/shard_map/dot_general | solution.py:29
  187.2 10.0 %fusion.58 = f32[128,4096]{1,0:T(8,128)S(1)} fusion(bf16[4096,1792]{1,0:T(8,128)(2,1)} %all-gather.5.cloned.1.call-done, bf16[128,896]{1,0:T(8,128)(2,1)S(1)} %get-tuple-element.29, bf16[128,896]{1,0:T(8,128)(2,1)S(1)} %get-tuple-element.28), kind=kOutput, calls=%fused_computation.91 | convolution fusion | flops 1879965696 | bytes 17235968 | tf_op jit(solution)/shard_map/dot_general | solution.py:231
  198.7 26.5 %attack_step.3.adversary_ref = f32[32,8,512]{2,1,0:T(8,128)S(1)} custom-call(f32[32,8,512]{2,1,0:T(8,128)S(1)} %bitcast.84, f32[32,8,512]{2,1,0:T(8,128)S(1)} %bitcast.82, f32[1]{0:T(128)} %get-tuple-element.40.step_ref), custom_call_target="tpu_custom_call" | custom-call | tf_op jit(solution)/shard_map/attack_step/pallas_call | solution.py:110
  226.3 7.3 %fusion.85 = f32[128,1792]{1,0:T(8,128)S(1)} fusion(bf16[128,4096]{1,0:T(8,128)(2,1)S(1)} %bitcast.129, bf16[4096,1792]{1,0:T(8,128)(2,1)} %all-gather.5.cloned.1.call-done), kind=kOutput, calls=%fused_computation.146 | convolution fusion | flops 1879048192 | bytes 16646144 | tf_op jit(solution)/shard_map/dot_general | solution.py:29
  233.8 10.2 %fusion.62 = f32[128,4096]{1,0:T(8,128)S(1)} fusion(bf16[4096,1792]{1,0:T(8,128)(2,1)} %all-gather.5.cloned.1.call-done, bf16[128,896]{1,0:T(8,128)(2,1)S(1)} %get-tuple-element.27, bf16[128,896]{1,0:T(8,128)(2,1)S(1)} %get-tuple-element.26), kind=kOutput, calls=%fused_computation.95 | convolution fusion | flops 1879965696 | bytes 17235968 | tf_op jit(solution)/shard_map/dot_general | solution.py:231
  245.5 24.5 %attack_step.4.adversary_ref = f32[32,8,512]{2,1,0:T(8,128)S(1)} custom-call(f32[32,8,512]{2,1,0:T(8,128)S(1)} %bitcast.85, f32[32,8,512]{2,1,0:T(8,128)S(1)} %attack_step.3.adversary_ref, f32[1]{0:T(128)} %get-tuple-element.41.step_ref), custom_call_target="tpu_custom_call" | custom-call | tf_op jit(solution)/shard_map/attack_step/pallas_call | solution.py:110
  271.1 7.3 %fusion.86 = f32[128,1792]{1,0:T(8,128)S(1)} fusion(bf16[128,4096]{1,0:T(8,128)(2,1)S(1)} %bitcast.130, bf16[4096,1792]{1,0:T(8,128)(2,1)} %all-gather.5.cloned.1.call-done), kind=kOutput, calls=%fused_computation.147 | convolution fusion | flops 1879048192 | bytes 16646144 | tf_op jit(solution)/shard_map/dot_general | solution.py:29
  278.7 10.0 %fusion.66 = f32[128,4096]{1,0:T(8,128)S(1)} fusion(bf16[4096,1792]{1,0:T(8,128)(2,1)} %all-gather.5.cloned.1.call-done, bf16[128,896]{1,0:T(8,128)(2,1)S(1)} %get-tuple-element.25, bf16[128,896]{1,0:T(8,128)(2,1)S(1)} %get-tuple-element.24), kind=kOutput, calls=%fused_computation.99 | convolution fusion | flops 1879965696 | bytes 17235968 | tf_op jit(solution)/shard_map/dot_general | solution.py:231
  290.2 24.0 %attack_step.5 = f32[32,8,512]{2,1,0:T(8,128)S(1)} custom-call(f32[32,8,512]{2,1,0:T(8,128)S(1)} %bitcast.83, f32[32,8,512]{2,1,0:T(8,128)S(1)} %attack_step.4.adversary_ref, f32[1]{0:T(128)} %get-tuple-element.39.step_ref), custom_call_target="tpu_custom_call" | custom-call | tf_op jit(solution)/shard_map/attack_step/pallas_call | solution.py:110
  314.7 10.4 %normed_rows.2 = bf16[4,256,4096]{2,1,0:T(8,128)(2,1)} custom-call(s32[4]{0:T(128)S(1)} %all-reduce.start_ref, bf16[4,256,4096]{2,1,0:T(8,128)(2,1)} %all-gather.7.cloned.1.call-done.state_ref, bf16[96,4096]{1,0:T(8,128)(2,1)S(1)} %pad_maximum_fusion.4.parts_ref, f32[1,4096]{1,0:T(1,128)S(1)} %bitcast.87), custom_call_target="tpu_custom_call" | custom-call | flops 838860800 | bytes 16777216 | tf_op jit(solution)/shard_map/normed_rows/pallas_call | solution.py:149
  325.1 19.2 %fusion.87 = f32[1024,1792]{1,0:T(8,128)S(1)} fusion(bf16[1024,4096]{1,0:T(8,128)(2,1)} %bitcast.123, bf16[4096,1792]{1,0:T(8,128)(2,1)} %all-gather.5.cloned.1.call-done), kind=kOutput, calls=%fused_computation.148 | convolution fusion | flops 15032385536 | bytes 30408704 | tf_op jit(solution)/shard_map/dot_general | solution.py:29
  344.3 4.8 fusion.1
  349.2 2.3 pad_maximum_fusion.1
  352.1 4.1 fusion.37
  356.2 3.4 fusion.40
  359.6 3.4 fusion.43
  363.1 10.0 %normed_rows.3 = bf16[4,256,4096]{2,1,0:T(8,128)(2,1)} custom-call(s32[4]{0:T(128)S(1)} %collective-permute-done.3.start_ref, bf16[4,256,4096]{2,1,0:T(8,128)(2,1)} %collective-permute-done.4.state_ref, bf16[96,4096]{1,0:T(8,128)(2,1)S(1)} %pad_maximum_fusion.4.parts_ref, f32[1,4096]{1,0:T(1,128)S(1)} %bitcast.88), custom_call_target="tpu_custom_call" | custom-call | flops 838860800 | bytes 16777216 | tf_op jit(solution)/shard_map/normed_rows/pallas_call | solution.py:149
  373.1 6.3 %multiply_reduce_fusion.1 = (f32[]{:T(128)}, bf16[512,1792]{1,0:T(8,128)(2,1)}) fusion(f32[512,1792]{1,0:T(8,128)S(1)} %fusion.37, bf16[1024,1792]{1,0:T(8,128)(2,1)} %collective-permute-done.5, bf16[1024,4096]{1,0:T(8,128)(2,1)} %bitcast.111, s32[]{:T(128)S(6)} %select_n.79), kind=kOutput, calls=%fused_computation.9 | convolution fusion | flops 1882718208 | bytes 10223624 | tf_op jit(solution)/shard_map/dot_general | solution.py:260
  379.4 1.6 collective-permute-start.8
  381.1 6.4 %multiply_reduce_fusion.3 = (f32[]{:T(128)}, bf16[512,1792]{1,0:T(8,128)(2,1)}) fusion(f32[512,1792]{1,0:T(8,128)S(1)} %fusion.40, bf16[1024,1792]{1,0:T(8,128)(2,1)} %collective-permute-done.5, bf16[1024,4096]{1,0:T(8,128)(2,1)} %bitcast.112, s32[]{:T(128)S(6)} %select_n.78), kind=kOutput, calls=%fused_computation.11 | convolution fusion | flops 1882718208 | bytes 10223624 | tf_op jit(solution)/shard_map/dot_general | solution.py:260
  387.4 1.5 collective-permute-start.7
  388.9 6.4 %multiply_reduce_fusion.2 = (f32[]{:T(128)}, bf16[512,1792]{1,0:T(8,128)(2,1)}) fusion(f32[512,1792]{1,0:T(8,128)S(1)} %fusion.43, bf16[1024,1792]{1,0:T(8,128)(2,1)} %collective-permute-done.5, bf16[1024,4096]{1,0:T(8,128)(2,1)} %bitcast.113, s32[]{:T(128)S(6)} %select_n.77), kind=kOutput, calls=%fused_computation.10 | convolution fusion | flops 1882718208 | bytes 10223624 | tf_op jit(solution)/shard_map/dot_general | solution.py:260
  395.5 5.8 %fusion.46 = f32[512,1792]{1,0:T(8,128)} fusion(bf16[1024,4096]{1,0:T(8,128)(2,1)} %bitcast.127, s32[]{:T(128)S(6)} %select_n.67, bf16[1024,896]{1,0:T(8,128)(2,1)} %copy-done.2, bf16[1024,896]{1,0:T(8,128)(2,1)S(1)} %get-tuple-element.2), kind=kOutput, calls=%fused_computation.67 | convolution fusion | flops 1886388224 | bytes 8388612 | tf_op jit(solution)/shard_map/dot_general | solution.py:257
  403.2 6.6 %multiply_reduce_fusion = (f32[]{:T(128)}, bf16[1,512,1792]{2,1,0:T(8,128)(2,1)S(1)}) fusion(f32[512,1792]{1,0:T(8,128)} %fusion.46, bf16[1024,1792]{1,0:T(8,128)(2,1)} %collective-permute-done.5, bf16[1024,4096]{1,0:T(8,128)(2,1)} %bitcast.114, s32[]{:T(128)S(6)} %select_n.67), kind=kOutput, calls=%fused_computation.8 | convolution fusion | flops 1882718208 | bytes 10223624 | tf_op jit(solution)/shard_map/dot_general | solution.py:260
  411.2 90.4 %psum.7 = f32[]{:T(128)} all-reduce(f32[]{:T(128)S(6)} %add.268), channel_id=1, replica_groups=mesh['tensor'=4,'dp'=4,'replica'=2] {'tensor','dp','replica'}, use_global_device_ids=true, to_apply=%region_13.14 | all-reduce | flops 1 | bytes 8 | tf_op jit(solution)/shard_map/psum | solution.py:267
  502.3 3.6 pad_maximum_fusion
  505.9 2.6 constant_dynamic-slice_fusion.3
  508.5 4.6 reshape.152
  513.1 4.6 reshape.151
  517.8 4.6 reshape.150
  522.4 1.5 reshape.149
  523.9 13.7 %multiply_convert_fusion = bf16[512,2,3584]{2,1,0:T(2,128)(2,1)} fusion(bf16[512,2,896]{2,1,0:T(2,128)(2,1)} %reshape.152, bf16[512,2,896]{2,1,0:T(2,128)(2,1)} %reshape.151, bf16[512,2,896]{2,1,0:T(2,128)(2,1)} %reshape.150, bf16[512,2,896]{2,1,0:T(2,128)(2,1)} %reshape.149, f32[]{:T(128)S(6)} %rsqrt.39), kind=kLoop, calls=%fused_computation | loop fusion | flops 36700160 | bytes 14680068 | tf_op jit(solution)/shard_map/convert_element_type | solution.py:277
  (83 shorter events, 14.5 us)
Async XLA Ops:
  7.2 54.1 %all-gather.9.cloned.1.call-start = ((), (), s32[]{:S(2)}) async-start(), calls=%async_computation.2 | async-start | bytes 2457600 | tf_op jit(solution)/shard_map/all_gather | solution.py:193
  10.8 139.3 %all-gather.7.cloned.1.call-start = ((), (), s32[]{:S(2)}) async-start(), calls=%async_computation.1 | async-start | bytes 10485760 | tf_op jit(solution)/shard_map/all_gather | solution.py:202
  11.6 167.8 %all-gather.5.cloned.1.call-start = ((), (), s32[]{:S(2)}) async-start(), calls=%async_computation | async-start | bytes 22020096 | tf_op jit(solution)/shard_map/all_gather | solution.py:181
  22.7 1.5 copy-start.4
  24.4 5.3 copy-start.12
  24.4 31.9 %copy-start.10 = (bf16[32,4096]{1,0:T(8,128)(2,1)S(1)}, bf16[32,4096]{1,0:T(8,128)(2,1)}, u32[]{:S(2)}) copy-start(bf16[32,4096]{1,0:T(8,128)(2,1)} %param.12) | copy-start | bytes 786436
  24.4 32.3 %copy-start.11 = (f32[3]{0:T(128)S(1)}, f32[3]{0:T(128)}, u32[]{:S(2)}) copy-start(f32[3]{0:T(128)} %param.13) | copy-start | bytes 40
  24.6 32.8 %collective-permute-start.2 = (bf16[256,896]{1,0:T(8,128)(2,1)S(1)}, bf16[256,896]{1,0:T(8,128)(2,1)S(1)}, u32[]{:S(2)}, u32[]{:S(2)}) collective-permute-start(bf16[256,896]{1,0:T(8,128)(2,1)S(1)} %get-tuple-element.21), channel_id=1, source_target_pairs={{0,6},{2,0},{4,2},{6,4},{1,7},{3,1},{5,3},{7,5},{8,14},{10,8},{12,... | collective-permute-start | bytes 1376264 | tf_op jit(solution)/shard_map/ppermute | solution.py:215
  28.5 28.8 %collective-permute-start.1 = (bf16[256,896]{1,0:T(8,128)(2,1)S(1)}, bf16[256,896]{1,0:T(8,128)(2,1)}, u32[]{:S(2)}, u32[]{:S(2)}) collective-permute-start(bf16[256,896]{1,0:T(8,128)(2,1)S(1)} %get-tuple-element.22), channel_id=1, source_target_pairs={{0,4},{2,6},{4,0},{6,2},{1,5},{3,7},{5,1},{7,3},{8,12},{10,14},{12... | collective-permute-start | bytes 1376264 | tf_op jit(solution)/shard_map/ppermute | solution.py:215
  29.0 28.3 %collective-permute-start = (bf16[256,896]{1,0:T(8,128)(2,1)S(1)}, bf16[256,896]{1,0:T(8,128)(2,1)}, u32[]{:S(2)}, u32[]{:S(2)}) collective-permute-start(bf16[256,896]{1,0:T(8,128)(2,1)S(1)} %get-tuple-element.23), channel_id=1, source_target_pairs={{0,2},{2,4},{4,6},{6,0},{1,3},{3,5},{5,7},{7,1},{8,10},{10,12},{12... | collective-permute-start | bytes 1376264 | tf_op jit(solution)/shard_map/ppermute | solution.py:215
  57.4 0.8 copy-start.9
  59.7 4.3 copy-start
  61.3 2.7 copy-start.1
  150.2 212.9 %collective-permute-start.4 = (bf16[4,256,4096]{2,1,0:T(8,128)(2,1)}, bf16[4,256,4096]{2,1,0:T(8,128)(2,1)}, u32[]{:S(2)}, u32[]{:S(2)}) collective-permute-start(bf16[4,256,4096]{2,1,0:T(8,128)(2,1)} %all-gather.7.cloned.1.call-done.state_ref), channel_id=1, source_target_pairs={{0,1},{1,0},{2,3},{3,2},{4,5},{5,4},{6,7},{7,6},{8,9},{9,8},{10,11... | collective-permute-start | bytes 25165832 | tf_op jit(solution)/shard_map/ppermute | solution.py:203
  325.1 19.2 %copy-start.5 = (bf16[256,896]{1,0:T(8,128)(2,1)S(1)}, bf16[256,896]{1,0:T(8,128)(2,1)}, u32[]{:S(2)}) copy-start(bf16[256,896]{1,0:T(8,128)(2,1)} %get-tuple-element.16) | copy-start | bytes 1376260
  325.1 19.2 %copy-start.6 = (bf16[256,896]{1,0:T(8,128)(2,1)S(1)}, bf16[256,896]{1,0:T(8,128)(2,1)}, u32[]{:S(2)}) copy-start(bf16[256,896]{1,0:T(8,128)(2,1)} %get-tuple-element.17) | copy-start | bytes 1376260
  325.1 19.2 %copy-start.7 = (bf16[256,896]{1,0:T(8,128)(2,1)S(1)}, bf16[256,896]{1,0:T(8,128)(2,1)}, u32[]{:S(2)}) copy-start(bf16[256,896]{1,0:T(8,128)(2,1)} %get-tuple-element.18) | copy-start | bytes 1376260
  325.1 19.2 %copy-start.8 = (bf16[256,896]{1,0:T(8,128)(2,1)S(1)}, bf16[256,896]{1,0:T(8,128)(2,1)}, u32[]{:S(2)}) copy-start(bf16[256,896]{1,0:T(8,128)(2,1)} %get-tuple-element.19) | copy-start | bytes 1376260
  349.1 2.4 copy-start.2
  351.5 21.6 %collective-permute-start.5 = (bf16[1024,1792]{1,0:T(8,128)(2,1)}, bf16[1024,1792]{1,0:T(8,128)(2,1)}, u32[]{:S(2)}, u32[]{:S(2)}) collective-permute-start(bf16[1024,1792]{1,0:T(8,128)(2,1)} %pad_maximum_fusion.1), channel_id=1, source_target_pairs={{0,1},{1,0},{2,3},{3,2},{4,5},{5,4},{6,7},{7,6},{8,9},{9,8},{10,11... | collective-permute-start | bytes 11010056 | tf_op jit(solution)/shard_map/ppermute | solution.py:248
  352.1 11.0 %collective-permute-start.3 = (s32[4]{0:T(128)S(1)}, s32[4]{0:T(128)S(1)}, u32[]{:S(2)}, u32[]{:S(2)}) collective-permute-start(s32[4]{0:T(128)S(1)} %all-reduce.start_ref), channel_id=1, source_target_pairs={{0,1},{1,0},{2,3},{3,2},{4,5},{5,4},{6,7},{7,6},{8,9},{9,8},{10,11... | collective-permute-start | bytes 56 | tf_op jit(solution)/shard_map/ppermute | solution.py:205
  352.1 4.1 copy-start.3
  379.4 122.9 %collective-permute-start.8 = (bf16[512,1792]{1,0:T(8,128)(2,1)}, bf16[512,1792]{1,0:T(8,128)(2,1)}, u32[]{:S(2)}, u32[]{:S(2)}) collective-permute-start(bf16[512,1792]{1,0:T(8,128)(2,1)} %get-tuple-element.11), channel_id=1, source_target_pairs={{0,6},{2,0},{4,2},{6,4},{1,7},{3,1},{5,3},{7,5},{8,14},{10,8},{12,... | collective-permute-start | bytes 5505032 | tf_op jit(solution)/shard_map/ppermute | solution.py:266
  387.4 114.9 %collective-permute-start.7 = (bf16[512,1792]{1,0:T(8,128)(2,1)}, bf16[512,1792]{1,0:T(8,128)(2,1)}, u32[]{:S(2)}, u32[]{:S(2)}) collective-permute-start(bf16[512,1792]{1,0:T(8,128)(2,1)} %get-tuple-element.15), channel_id=1, source_target_pairs={{0,4},{2,6},{4,0},{6,2},{1,5},{3,7},{5,1},{7,3},{8,12},{10,14},{12... | collective-permute-start | bytes 5505032 | tf_op jit(solution)/shard_map/ppermute | solution.py:266
  395.3 107.0 %collective-permute-start.6 = (bf16[512,1792]{1,0:T(8,128)(2,1)}, bf16[512,1792]{1,0:T(8,128)(2,1)}, u32[]{:S(2)}, u32[]{:S(2)}) collective-permute-start(bf16[512,1792]{1,0:T(8,128)(2,1)} %get-tuple-element.13), channel_id=1, source_target_pairs={{0,2},{2,4},{4,6},{6,0},{1,3},{3,5},{5,7},{7,1},{8,10},{10,12},{12... | collective-permute-start | bytes 5505032 | tf_op jit(solution)/shard_map/ppermute | solution.py:266
Sparse Core Ops, SparseCore 0:
  11.0 50.2 all-gather.8
  63.1 86.9 all-gather.6
  152.3 27.0 all-gather.4

commit v2 on v1

--- a/solution.py
+++ b/solution.py
@@ -121,12 +121,75 @@
             compiler_params=pltpu.CompilerParams(
                 collective_id=0, has_side_effects=True, vmem_limit_bytes=16 << 20
             ),
+            cost_estimate=pl.CostEstimate(
+                flops=20_000_000_000, bytes_accessed=3 * count * width * 4, transcendentals=0
+            ),
             name="attack_step",
         )(partial.reshape(shape), adversary.reshape(shape), step_size)
         return result.reshape(count, width)
     grad = lax.psum(partial, ("tensor", "dp", "replica"))
     scale = lax.rsqrt(jnp.mean(grad * grad, axis=-1, keepdims=True) + 1e-06)
     return adversary + step_size[0] * grad * scale
+
+
+def scalar_kernel(tensors, chips, cores, value_ref, out_ref, buf1, buf2, mine, send1, recv1, send2, recv2):
+    group = chips * cores
+    t = lax.axis_index("tensor")
+    g = lax.axis_index("dp") * cores + lax.axis_index("replica")
+    plane = [lax.rem(g + k, group) for k in range(1, group)]
+    plane_ids = [{"dp": p // cores, "replica": lax.rem(p, cores)} for p in plane]
+    line_ids = [{"tensor": lax.rem(t + k, tensors)} for k in range(1, tensors)]
+    barrier = pltpu.get_barrier_semaphore()
+    for device in plane_ids + line_ids:
+        pl.semaphore_signal(barrier, inc=1, device_id=device, device_id_type=MESH)
+    pl.semaphore_wait(barrier, group + tensors - 2)
+    copies = []
+    total = value_ref[...]
+    source = value_ref
+    for ids, buf, sends, recvs in ((plane_ids, buf1, send1, recv1), (line_ids, buf2, send2, recv2)):
+        stage = []
+        for k, device in enumerate(ids):
+            copy = pltpu.make_async_remote_copy(
+                src_ref=source, dst_ref=buf.at[k], send_sem=sends.at[k], recv_sem=recvs.at[k],
+                device_id=device, device_id_type=MESH,
+            )
+            copy.start()
+            stage.append(copy)
+        for k, copy in enumerate(stage):
+            copy.wait_recv()
+            total = total + buf[k]
+        copies += stage
+        if buf is buf1:
+            mine[...] = total
+            source = mine
+    out_ref[...] = total
+    for copy in copies:
+        copy.wait_send()
+
+
+def sum_everywhere(value):
+    tensors, chips, cores = (lax.axis_size(a) for a in ("tensor", "dp", "replica"))
+    group = chips * cores
+    if not 1 < tensors <= 8 or not 1 < group <= 16:
+        return lax.psum(value, ("tensor", "dp", "replica"))
+    dma = pltpu.SemaphoreType.DMA
+    vmem = pl.BlockSpec(memory_space=pltpu.VMEM)
+    return pl.pallas_call(
+        functools.partial(scalar_kernel, tensors, chips, cores),
+        out_shape=jax.ShapeDtypeStruct((8, 128), jnp.float32),
+        in_specs=[vmem],
+        out_specs=vmem,
+        scratch_shapes=[
+            pltpu.VMEM((group - 1, 8, 128), jnp.float32),
+            pltpu.VMEM((tensors - 1, 8, 128), jnp.float32),
+            pltpu.VMEM((8, 128), jnp.float32),
+        ]
+        + [dma((group - 1,))] * 2 + [dma((tensors - 1,))] * 2,
+        compiler_params=pltpu.CompilerParams(
+            collective_id=1, has_side_effects=True, vmem_limit_bytes=4 << 20
+        ),
+        name="scalar_sum",
+    )(jnp.full((8, 128), value, jnp.float32))[0, 0]
 
 
 def norm_kernel(start_ref, state_ref, parts_ref, gain_ref, out_ref):
@@ -187,6 +250,7 @@
         [
             lax.dynamic_slice_in_dim(seq_states, prompt_start, count, 0),
             lax.dynamic_slice_in_dim(seq_cotan, prompt_start, count, 0),
+            jnp.broadcast_to(insert_at.astype(jnp.bfloat16).reshape(1, 1), (count, 128)),
         ],
         axis=1,
     )
@@ -199,9 +263,9 @@
     )
 
     swap = [(i, (i + 1) % cores) for i in range(cores)]
+    own_starts = package[:, 0, package.shape[2] - 1].astype(jnp.int32)
+    seq_states, seq_cotan, _ = lax.optimization_barrier((seq_states, seq_cotan, weight_pair))
     own_states = lax.all_gather(seq_states, "dp", axis=0, tiled=False)
-    other_states = lax.ppermute(own_states, "replica", swap)
-    own_starts = lax.all_gather(insert_at, "dp", axis=0, tiled=True)
     other_starts = lax.ppermute(own_starts, "replica", swap)
     positions = lax.broadcasted_iota(jnp.int32, (tokens, 1), 0)
     live_cotan = jnp.where(positions < lengths[0], seq_cotan, jnp.zeros_like(seq_cotan))
@@ -238,6 +302,9 @@
             axis=0,
         )
         adversary = apply_step(partial, adversary, step_sizes[attack_step : attack_step + 1])
+        if attack_step == step_sizes.shape[0] - 2:
+            own_states, adversary = lax.optimization_barrier((own_states, adversary))
+            other_states = lax.ppermute(own_states, "replica", swap)
 
     high = lax.reduce_precision(adversary, 8, 7)
     middle = lax.reduce_precision(adversary - high, 8, 7)
@@ -262,9 +329,9 @@
             preferred_element_type=jnp.float32,
         )
         squares = squares + jnp.sum(block * block)
-        sent = block.astype(jnp.bfloat16)
+        sent = block.astype(jnp.bfloat16).reshape(block_width, 2, units)
         received[k] = lax.ppermute(sent, "dp", shifted_perm(k)) if k else sent
-    squares = lax.psum(squares, ("tensor", "dp", "replica"))
+    squares = sum_everywhere(squares)
     scale = lax.rsqrt(squares / (2 * D * FF) + 1e-06)
     stacked = jnp.stack(received)
     pieces = [
@@ -272,7 +339,7 @@
         for j in range(chips)
     ]
     weight_step = jnp.concatenate(
-        [piece.reshape(block_width, 2, units) for piece in pieces], axis=2
+        pieces, axis=2
     )
     weight_step = (weight_step.astype(jnp.float32) * scale).astype(jnp.bfloat16)
     column_count = width // lax.axis_size("tensor")

time: 549 us -> 500 us (0.911)
  blocking collectives: 116 us -> 0 us
  Pallas kernels: 95.4 us -> 195 us
  waiting for transfers between devices: 115 us -> 51.2 us
  other arithmetic: 36 us -> 65.3 us
    psum x1 -> x0, blocking collectives: 90.4 us -> none  [per_device(): squares = lax.psum(squares, ('tensor', 'dp', 'replica'))]
    all_gather x1, waiting for transfers between devices: 84.8 us -> 0.01 us  [per_device(): own_states = lax.all_gather(seq_states, 'dp', axis=0, tiled=False)]
    pallas_call x0 -> x1, Pallas kernels: none -> 53.7 us  [sum_everywhere(): pl.pallas_call(functools.partial(scalar_kernel, tensors, chips, cores), o...]
    pallas_call x3, Pallas kernels: 75 us -> 120 us  [apply_step(): pl.pallas_call(functools.partial(step_kernel, tensors, chips, cores), out...]
    unnamed x1 -> x0, blocking collectives: 25.2 us -> none
    all_gather x1, waiting for transfers between devices: 0.27 us -> 23.7 us  [per_device(): package = lax.all_gather(package, 'dp', axis=0, tiled=False)]
    convert_element_type x1, other arithmetic: 13.7 us -> 33.5 us  [per_device(): weight_step = (weight_step.astype(jnp.float32) * scale).astype(jnp.bfloat16)]
    another operation x1, other arithmetic: 3.59 us -> 14.9 us  [per_device(): stacked = jnp.stack(received)]
  transfers between devices with their start and end apart: 12 -> 12, of which waited for: 3 -> 2; matrix products, arithmetic and copies ran while one was open for 26% -> 27% of each run, Pallas kernels for 18% -> 34%
where the time goes in v2:
time: 500 us; the launch traced here: 496 us
  Pallas kernels  195 us (39%)
  matrix products  115 us (23%)
  other arithmetic  65.3 us (13%)
  waiting for transfers between devices  51.2 us (10%)
  local copies, waits for them, and re-layouts  42.9 us (9%)
  between operations  19.1 us (4%)
  starting transfers between devices  8.8 us (2%)
    pallas_call x3, Pallas kernels, apply_step(): pl.pallas_call(functools.partial(step_kernel, tensors, chips, cores), out...  120 us
    pallas_call x1, Pallas kernels, sum_everywhere(): pl.pallas_call(functools.partial(scalar_kernel, tensors, chips, cores), o...  53.7 us
    dot_general x4, matrix products, hidden_grads(): jnp.dot(normalized, weight_pair, preferred_element_type=jnp.float32)  35.8 us
    convert_element_type x1, other arithmetic, per_device(): weight_step = (weight_step.astype(jnp.float32) * scale).astype(jnp.bfloat16)  33.5 us
    dot_general x3, matrix products, per_device(): lax.dot_general(unit_grads, weight_pair, (((1,), (1,)), ((), ())), prefer...  32.3 us
    dot_general x4, matrix products, per_device(): lax.dot_general(lax.dynamic_slice_in_dim(other_normed, start, block_width...  27.9 us
    all_gather x1, waiting for transfers between devices, per_device(): lax.all_gather(unit_slice.reshape(half, 2 * units), 'replica', axis=0, ti...  27.4 us
    all_gather x1, waiting for transfers between devices, per_device(): package = lax.all_gather(package, 'dp', axis=0, tiled=False)  23.7 us
  transfers between devices with their start and end apart: 12, of which 2 were waited for; matrix products, arithmetic and copies ran while one was open for 27% of the time, Pallas kernels for 34%

profile of v2, /device:TPU:0, one launch (start us, length us, event | category | flops | bytes accessed | tf_op | source)
XLA Modules:
  0.0 496.5 jit_solution(5169403910124464460)
XLA Ops:
  7.9 1.0 dynamic-slice_bitcast_fusion.10
  8.9 1.0 dynamic-slice_bitcast_fusion.9
  9.9 0.9 maximum_maximum_fusion
  10.9 6.5 %constant_dynamic-slice_fusion.5 = bf16[2048,2,896]{2,1,0:T(2,128)(2,1)S(1)} fusion(bf16[2048,2,3584]{2,1,0:T(2,128)(2,1)} %param.10, s32[]{:T(128)S(6)} %select_n.64), kind=kLoop, calls=%fused_computation.129 | loop fusion | bytes 14680068 | tf_op jit(solution)/shard_map/dynamic_slice | solution.py:243
  17.4 4.6 copy.14
  22.2 0.7 copy-done.9
  24.6 23.7 %all-gather.8.cloned.1.call-done = bf16[128,7808]{1,0:T(8,128)(2,1)} async-done(((bf16[32,7808]{1,0:T(8,128)(2,1)}), bf16[128,7808]{1,0:T(8,128)(2,1)}) %all-gather.8.cloned.1.call-update) | async-done | bytes 1998864 | tf_op jit(solution)/shard_map/all_gather | solution.py:257
  48.2 1.7 fusion.29
  50.0 27.4 %all-gather.6.cloned.1.call-done = bf16[4096,1792]{1,0:T(8,128)(2,1)} async-done(((bf16[2048,1792]{1,0:T(8,128)(2,1)}), bf16[4096,1792]{1,0:T(8,128)(2,1)}) %all-gather.6.cloned.1.call-update) | async-done | bytes 14680080 | tf_op jit(solution)/shard_map/all_gather | solution.py:244
  78.1 7.3 %fusion.83 = f32[128,1792]{1,0:T(8,128)S(1)} fusion(bf16[128,4096]{1,0:T(8,128)(2,1)S(1)} %bitcast.142, bf16[4096,1792]{1,0:T(8,128)(2,1)} %all-gather.6.cloned.1.call-done), kind=kOutput, calls=%fused_computation.146 | convolution fusion | flops 1879048192 | bytes 16646144 | tf_op jit(solution)/shard_map/dot_general | solution.py:29
  85.6 12.1 %fusion.58 = f32[128,4096]{1,0:T(8,128)S(1)} fusion(bf16[4096,1792]{1,0:T(8,128)(2,1)} %all-gather.6.cloned.1.call-done, bf16[128,896]{1,0:T(8,128)(2,1)S(1)} %get-tuple-element.37, bf16[128,896]{1,0:T(8,128)(2,1)S(1)} %get-tuple-element.36), kind=kOutput, calls=%fused_computation.94 | convolution fusion | flops 1879965696 | bytes 17235968 | tf_op jit(solution)/shard_map/dot_general | solution.py:295
  98.3 0.7 fusion.34
  99.3 33.3 %attack_step.3.adversary_ref = f32[32,8,512]{2,1,0:T(8,128)S(1)} custom-call(f32[32,8,512]{2,1,0:T(8,128)S(1)} %bitcast.97, f32[32,8,512]{2,1,0:T(8,128)S(1)} %bitcast.92, f32[1]{0:T(128)} %get-tuple-element.48.step_ref), custom_call_target="tpu_custom_call" | custom-call | flops 20000000000 | bytes 1572864 | tf_op jit(solution)/shard_map/attack_step/pallas_call | solution.py:110
  133.7 2.1 fusion.84
  136.1 10.2 %fusion.62 = f32[128,4096]{1,0:T(8,128)S(1)} fusion(bf16[4096,1792]{1,0:T(8,128)(2,1)} %all-gather.6.cloned.1.call-done, bf16[128,896]{1,0:T(8,128)(2,1)S(1)} %get-tuple-element.35, bf16[128,896]{1,0:T(8,128)(2,1)S(1)} %get-tuple-element.34), kind=kOutput, calls=%fused_computation.98 | convolution fusion | flops 1879965696 | bytes 17235968 | tf_op jit(solution)/shard_map/dot_general | solution.py:295
  146.9 0.7 fusion.27
  148.8 1.9 collective-permute-start.2
  150.6 1.8 collective-permute-start.1
  152.4 63.3 %attack_step.4 = f32[32,8,512]{2,1,0:T(8,128)S(1)} custom-call(f32[32,8,512]{2,1,0:T(8,128)S(1)} %bitcast.94, f32[32,8,512]{2,1,0:T(8,128)S(1)} %attack_step.3.adversary_ref, f32[1]{0:T(128)} %get-tuple-element.49.step_ref), custom_call_target="tpu_custom_call" | custom-call | flops 20000000000 | bytes 1572864 | tf_op jit(solution)/shard_map/attack_step/pallas_call | solution.py:110
  216.3 1.3 dynamic-slice_bitcast_fusion.7
  218.3 7.3 %fusion.85 = f32[128,1792]{1,0:T(8,128)S(1)} fusion(bf16[128,4096]{1,0:T(8,128)(2,1)S(1)} %bitcast.144, bf16[4096,1792]{1,0:T(8,128)(2,1)} %all-gather.6.cloned.1.call-done), kind=kOutput, calls=%fused_computation.148 | convolution fusion | flops 1879048192 | bytes 16646144 | tf_op jit(solution)/shard_map/dot_general | solution.py:29
  225.8 10.0 %fusion.66 = f32[128,4096]{1,0:T(8,128)S(1)} fusion(bf16[4096,1792]{1,0:T(8,128)(2,1)} %all-gather.6.cloned.1.call-done, bf16[128,896]{1,0:T(8,128)(2,1)S(1)} %get-tuple-element.33, bf16[128,896]{1,0:T(8,128)(2,1)S(1)} %get-tuple-element.32), kind=kOutput, calls=%fused_computation.102 | convolution fusion | flops 1879965696 | bytes 17235968 | tf_op jit(solution)/shard_map/dot_general | solution.py:295
  236.4 0.7 fusion.20
  237.7 23.9 %attack_step.5 = f32[32,8,512]{2,1,0:T(8,128)S(1)} custom-call(f32[32,8,512]{2,1,0:T(8,128)S(1)} %bitcast.95, f32[32,8,512]{2,1,0:T(8,128)S(1)} %bitcast.96, f32[1]{0:T(128)} %get-tuple-element.47.step_ref), custom_call_target="tpu_custom_call" | custom-call | flops 20000000000 | bytes 1572864 | tf_op jit(solution)/shard_map/attack_step/pallas_call | solution.py:110
  262.8 10.4 %normed_rows.2 = bf16[4,256,4096]{2,1,0:T(8,128)(2,1)} custom-call(s32[4]{0:T(128)S(1)} %fusion.78.start_ref, bf16[4,256,4096]{2,1,0:T(8,128)(2,1)} %bitcast.7.state_ref, bf16[96,4096]{1,0:T(8,128)(2,1)S(1)} %pad_maximum_fusion.4.parts_ref, f32[1,4096]{1,0:T(1,128)S(1)} %bitcast.90), custom_call_target="tpu_custom_call" | custom-call | flops 838860800 | bytes 16777216 | tf_op jit(solution)/shard_map/normed_rows/pallas_call | solution.py:212
  273.2 19.2 %fusion.86 = f32[1024,1792]{1,0:T(8,128)S(1)} fusion(bf16[1024,4096]{1,0:T(8,128)(2,1)} %bitcast.137, bf16[4096,1792]{1,0:T(8,128)(2,1)} %all-gather.6.cloned.1.call-done), kind=kOutput, calls=%fused_computation.149 | convolution fusion | flops 15032385536 | bytes 30408704 | tf_op jit(solution)/shard_map/dot_general | solution.py:29
  292.4 4.8 fusion.1
  297.2 2.3 pad_maximum_fusion.1
  300.1 4.0 fusion.37
  304.2 5.3 %fusion.40 = f32[512,1792]{1,0:T(8,128)} fusion(bf16[1024,4096]{1,0:T(8,128)(2,1)} %bitcast.139, s32[]{:T(128)S(6)} %select_n.78, bf16[1024,896]{1,0:T(8,128)(2,1)S(1)} %copy-done.3, bf16[1024,896]{1,0:T(8,128)(2,1)S(1)} %get-tuple-element.10), kind=kOutput, calls=%fused_computation.64 | convolution fusion | flops 1886388224 | bytes 8388612 | tf_op jit(solution)/shard_map/dot_general | solution.py:324
  309.5 5.2 %fusion.43 = f32[512,1792]{1,0:T(8,128)} fusion(bf16[1024,4096]{1,0:T(8,128)(2,1)} %bitcast.140, s32[]{:T(128)S(6)} %select_n.77, bf16[1024,896]{1,0:T(8,128)(2,1)S(1)} %copy-done.3, bf16[1024,896]{1,0:T(8,128)(2,1)S(1)} %get-tuple-element.10), kind=kOutput, calls=%fused_computation.67 | convolution fusion | flops 1886388224 | bytes 8388612 | tf_op jit(solution)/shard_map/dot_general | solution.py:324
  314.7 10.0 %normed_rows.3 = bf16[4,256,4096]{2,1,0:T(8,128)(2,1)} custom-call(s32[4]{0:T(128)S(1)} %collective-permute-done.3.start_ref, bf16[4,256,4096]{2,1,0:T(8,128)(2,1)} %collective-permute-done.4.state_ref, bf16[96,4096]{1,0:T(8,128)(2,1)S(1)} %pad_maximum_fusion.4.parts_ref, f32[1,4096]{1,0:T(1,128)S(1)} %bitcast.91), custom_call_target="tpu_custom_call" | custom-call | flops 838860800 | bytes 16777216 | tf_op jit(solution)/shard_map/normed_rows/pallas_call | solution.py:212
  324.7 6.5 %multiply_reduce_fusion.1 = (f32[]{:T(128)}, bf16[512,1792]{1,0:T(8,128)(2,1)}) fusion(f32[512,1792]{1,0:T(8,128)S(1)} %fusion.37, bf16[1024,1792]{1,0:T(8,128)(2,1)} %collective-permute-done.5, bf16[1024,4096]{1,0:T(8,128)(2,1)} %bitcast.129, s32[]{:T(128)S(6)} %select_n.79), kind=kOutput, calls=%fused_computation.9 | convolution fusion | flops 1882718208 | bytes 10223624 | tf_op jit(solution)/shard_map/dot_general | solution.py:327
  331.2 4.6 reshape.161
  335.9 1.9 collective-permute-start.8
  337.8 7.4 %multiply_reduce_fusion.3 = (f32[]{:T(128)}, bf16[512,1792]{1,0:T(8,128)(2,1)}) fusion(f32[512,1792]{1,0:T(8,128)} %fusion.40, bf16[1024,1792]{1,0:T(8,128)(2,1)} %collective-permute-done.5, bf16[1024,4096]{1,0:T(8,128)(2,1)} %bitcast.130, s32[]{:T(128)S(6)} %select_n.78), kind=kOutput, calls=%fused_computation.11 | convolution fusion | flops 1882718208 | bytes 10223624 | tf_op jit(solution)/shard_map/dot_general | solution.py:327
  345.3 4.6 reshape.160
  349.9 1.2 collective-permute-start.7
  351.1 7.5 %multiply_reduce_fusion.2 = (f32[]{:T(128)}, bf16[512,1792]{1,0:T(8,128)(2,1)}) fusion(f32[512,1792]{1,0:T(8,128)} %fusion.43, bf16[1024,1792]{1,0:T(8,128)(2,1)} %collective-permute-done.5, bf16[1024,4096]{1,0:T(8,128)(2,1)} %bitcast.131, s32[]{:T(128)S(6)} %select_n.77), kind=kOutput, calls=%fused_computation.10 | convolution fusion | flops 1882718208 | bytes 10223624 | tf_op jit(solution)/shard_map/dot_general | solution.py:327
  358.6 4.6 reshape.159
  363.8 0.7 constant_dynamic-slice_fusion.3
  364.5 4.0 fusion.46
  368.5 6.5 %multiply_reduce_fusion = (f32[]{:T(128)}, bf16[512,1792]{1,0:T(8,128)(2,1)}) fusion(f32[512,1792]{1,0:T(8,128)S(1)} %fusion.46, bf16[1024,1792]{1,0:T(8,128)(2,1)} %collective-permute-done.5, bf16[1024,4096]{1,0:T(8,128)(2,1)} %bitcast.132, s32[]{:T(128)S(6)} %select_n.67), kind=kOutput, calls=%fused_computation.8 | convolution fusion | flops 1882718208 | bytes 10223624 | tf_op jit(solution)/shard_map/dot_general | solution.py:327
  375.0 3.8 stack_reshape.3
  381.2 53.7 %scalar_sum.1 = f32[8,128]{1,0:T(8,128)S(1)} custom-call(f32[8,128]{1,0:T(8,128)S(1)} %broadcast_in_dim.20.value_ref), custom_call_target="tpu_custom_call" | custom-call | tf_op jit(solution)/shard_map/scalar_sum/pallas_call | solution.py:177
  436.1 14.9 %pad_maximum_fusion = bf16[4,512,2,896]{3,2,1,0:T(2,128)(2,1)S(1)} fusion(bf16[1,512,2,896]{3,2,1,0:T(2,128)(2,1)} %bitcast.30, bf16[1,512,2,896]{3,2,1,0:T(2,128)(2,1)} %bitcast.29, bf16[1,512,2,896]{3,2,1,0:T(2,128)(2,1)} %bitcast.28, bf16[1,512,2,896]{3,2,1,0:T(2,128)(2,1)S(1)} %stack_reshape.3), kind=kLoop, calls=%fused_computation.1 | loop fusion | flops 11010048 | bytes 14680064 | tf_op jit(solution)/shard_map/stack | solution.py:336
  451.0 5.1 %dynamic-slice_bitcast_fusion.3 = (bf16[512,2,896]{2,1,0:T(2,128)(2,1)S(1)}, bf16[512,2,896]{2,1,0:T(2,128)(2,1)S(1)}, bf16[512,2,896]{2,1,0:T(2,128)(2,1)S(1)}, bf16[512,2,896]{2,1,0:T(2,128)(2,1)S(1)}) fusion(bf16[4,512,2,896]{3,2,1,0:T(2,128)(2,1)S(1)} %pad_maximum_fusion, s32[]{:T(128)S(6)} %select_n.73, s32[]{:T(128)S(6)} %select_n.76, ...), kind=kLoop, calls=%fused_computation.58 | loop fusion | bytes 14680080 | tf_op jit(solution)/shard_map/jit(dynamic_index_in_dim)/squeeze | solution.py:338
  456.2 33.5 %multiply_convert_fusion = bf16[512,2,3584]{2,1,0:T(2,128)(2,1)} fusion(bf16[512,2,896]{2,1,0:T(2,128)(2,1)S(1)} %get-tuple-element.13, bf16[512,2,896]{2,1,0:T(2,128)(2,1)S(1)} %get-tuple-element.14, bf16[512,2,896]{2,1,0:T(2,128)(2,1)S(1)} %get-tuple-element.15, bf16[512,2,896]{2,1,0:T(2,128)(2,1)S(1)} %get-tuple-element.12, f32[]{:T(128)} %bitcast.35), kind=kLoop, calls=%fused_computation | loop fusion | flops 36700160 | bytes 14680068 | tf_op jit(solution)/shard_map/convert_element_type | solution.py:344
  (90 shorter events, 11.8 us)
Async XLA Ops:
  7.2 41.1 %all-gather.8.cloned.1.call-start = ((), (), s32[]{:S(2)}) async-start(), calls=%async_computation.1 | async-start | bytes 2498560 | tf_op jit(solution)/shard_map/all_gather | solution.py:257
  10.8 66.6 %all-gather.6.cloned.1.call-start = ((), (), s32[]{:S(2)}) async-start(), calls=%async_computation | async-start | bytes 22020096 | tf_op jit(solution)/shard_map/all_gather | solution.py:244
  21.9 1.0 copy-start.9
  21.9 2.0 copy-start.10
  22.0 195.6 %all-gather.10.cloned.1.call-start = ((), (), s32[]{:S(2)}) async-start(), calls=%async_computation.2 | async-start | bytes 10485760 | tf_op jit(solution)/shard_map/all_gather | solution.py:268
  23.2 54.2 %copy-start = (f32[4096]{0:T(1024)S(1)}, f32[4096]{0:T(1024)}, u32[]{:S(2)}) copy-start(f32[4096]{0:T(1024)} %param.9) | copy-start | bytes 49156
  48.2 29.2 %copy-start.1 = (bf16[128,7808]{1,0:T(8,128)(2,1)S(1)}, bf16[128,7808]{1,0:T(8,128)(2,1)}, u32[]{:S(2)}) copy-start(bf16[128,7808]{1,0:T(8,128)(2,1)} %all-gather.8.cloned.1.call-done) | copy-start | bytes 5996548
  98.3 35.4 %slice-start = ((s8[14680064]{0:T(1024)(128)(4,1)}), s8[4194304]{0:T(1024)(128)(4,1)S(1)}, s32[]{:S(2)}) async-start(s8[14680064]{0:T(1024)(128)(4,1)} %bitcast.100), calls=%async_computation.3 | async-start | bytes 8388608
  99.3 34.4 %slice-start.1 = ((s8[14680064]{0:T(1024)(128)(4,1)}), s8[4194304]{0:T(1024)(128)(4,1)S(1)}, s32[]{:S(2)}) async-start(s8[14680064]{0:T(1024)(128)(4,1)} %bitcast.100), calls=%async_computation.4 | async-start | bytes 8388608
  99.3 34.4 %slice-start.2 = ((s8[14680064]{0:T(1024)(128)(4,1)}), s8[4194304]{0:T(1024)(128)(4,1)S(1)}, s32[]{:S(2)}) async-start(s8[14680064]{0:T(1024)(128)(4,1)} %bitcast.100), calls=%async_computation.5 | async-start | bytes 8388608
  99.3 34.4 %slice-start.3 = ((s8[14680064]{0:T(1024)(128)(4,1)}), s8[2097152]{0:T(1024)(128)(4,1)S(1)}, s32[]{:S(2)}) async-start(s8[14680064]{0:T(1024)(128)(4,1)} %bitcast.100), calls=%async_computation.6 | async-start | bytes 4194304
  146.9 1.5 copy-start.4
  148.8 67.2 %collective-permute-start.2 = (bf16[256,896]{1,0:T(8,128)(2,1)S(1)}, bf16[256,896]{1,0:T(8,128)(2,1)S(1)}, u32[]{:S(2)}, u32[]{:S(2)}) collective-permute-start(bf16[256,896]{1,0:T(8,128)(2,1)S(1)} %get-tuple-element.29), channel_id=1, source_target_pairs={{0,6},{2,0},{4,2},{6,4},{1,7},{3,1},{5,3},{7,5},{8,14},{10,8},{12,... | collective-permute-start | bytes 1376264 | tf_op jit(solution)/shard_map/ppermute | solution.py:279
  150.6 65.4 %collective-permute-start.1 = (bf16[256,896]{1,0:T(8,128)(2,1)S(1)}, bf16[256,896]{1,0:T(8,128)(2,1)S(1)}, u32[]{:S(2)}, u32[]{:S(2)}) collective-permute-start(bf16[256,896]{1,0:T(8,128)(2,1)S(1)} %get-tuple-element.30), channel_id=1, source_target_pairs={{0,4},{2,6},{4,0},{6,2},{1,5},{3,7},{5,1},{7,3},{8,12},{10,14},{12... | collective-permute-start | bytes 1376264 | tf_op jit(solution)/shard_map/ppermute | solution.py:279
  152.4 63.6 %collective-permute-start = (bf16[256,896]{1,0:T(8,128)(2,1)S(1)}, bf16[256,896]{1,0:T(8,128)(2,1)S(1)}, u32[]{:S(2)}, u32[]{:S(2)}) collective-permute-start(bf16[256,896]{1,0:T(8,128)(2,1)S(1)} %get-tuple-element.31), channel_id=1, source_target_pairs={{0,2},{2,4},{4,6},{6,0},{1,3},{3,5},{5,7},{7,1},{8,10},{10,12},{12... | collective-permute-start | bytes 1376264 | tf_op jit(solution)/shard_map/ppermute | solution.py:279
  262.1 52.6 %collective-permute-start.4 = (bf16[4,256,4096]{2,1,0:T(8,128)(2,1)}, bf16[4,256,4096]{2,1,0:T(8,128)(2,1)}, u32[]{:S(2)}, u32[]{:S(2)}) collective-permute-start(bf16[4,256,4096]{2,1,0:T(8,128)(2,1)} %bitcast.7.state_ref), channel_id=1, source_target_pairs={{0,1},{1,0},{2,3},{3,2},{4,5},{5,4},{6,7},{7,6},{8,9},{9,8},{10,11... | collective-permute-start | bytes 25165832 | tf_op jit(solution)/shard_map/ppermute | solution.py:307
  273.2 19.2 %copy-start.5 = (bf16[256,896]{1,0:T(8,128)(2,1)S(1)}, bf16[256,896]{1,0:T(8,128)(2,1)}, u32[]{:S(2)}) copy-start(bf16[256,896]{1,0:T(8,128)(2,1)} %get-tuple-element.24) | copy-start | bytes 1376260
  273.2 19.2 %copy-start.6 = (bf16[256,896]{1,0:T(8,128)(2,1)S(1)}, bf16[256,896]{1,0:T(8,128)(2,1)}, u32[]{:S(2)}) copy-start(bf16[256,896]{1,0:T(8,128)(2,1)} %get-tuple-element.25) | copy-start | bytes 1376260
  273.2 19.2 %copy-start.7 = (bf16[256,896]{1,0:T(8,128)(2,1)S(1)}, bf16[256,896]{1,0:T(8,128)(2,1)}, u32[]{:S(2)}) copy-start(bf16[256,896]{1,0:T(8,128)(2,1)} %get-tuple-element.26) | copy-start | bytes 1376260
  273.2 19.2 %copy-start.8 = (bf16[256,896]{1,0:T(8,128)(2,1)S(1)}, bf16[256,896]{1,0:T(8,128)(2,1)}, u32[]{:S(2)}) copy-start(bf16[256,896]{1,0:T(8,128)(2,1)} %get-tuple-element.27) | copy-start | bytes 1376260
  297.2 2.4 copy-start.2
  299.6 25.1 %collective-permute-start.5 = (bf16[1024,1792]{1,0:T(8,128)(2,1)}, bf16[1024,1792]{1,0:T(8,128)(2,1)}, u32[]{:S(2)}, u32[]{:S(2)}) collective-permute-start(bf16[1024,1792]{1,0:T(8,128)(2,1)} %pad_maximum_fusion.1), channel_id=1, source_target_pairs={{0,1},{1,0},{2,3},{3,2},{4,5},{5,4},{6,7},{7,6},{8,9},{9,8},{10,11... | collective-permute-start | bytes 11010056 | tf_op jit(solution)/shard_map/ppermute | solution.py:315
  299.6 4.6 copy-start.3
  299.6 15.1 %collective-permute-start.3 = (s32[4]{0:T(128)S(1)}, s32[4]{0:T(128)S(1)}, u32[]{:S(2)}, u32[]{:S(2)}) collective-permute-start(s32[4]{0:T(128)S(1)} %fusion.78.start_ref), channel_id=1, source_target_pairs={{0,1},{1,0},{2,3},{3,2},{4,5},{5,4},{6,7},{7,6},{8,9},{9,8},{10,11... | collective-permute-start | bytes 56 | tf_op jit(solution)/shard_map/ppermute | solution.py:269
  335.9 100.2 %collective-permute-start.8 = (bf16[512,2,896]{2,1,0:T(2,128)(2,1)}, bf16[512,2,896]{2,1,0:T(2,128)(2,1)}, u32[]{:S(2)}, u32[]{:S(2)}) collective-permute-start(bf16[512,2,896]{2,1,0:T(2,128)(2,1)} %reshape.161), channel_id=1, source_target_pairs={{0,6},{2,0},{4,2},{6,4},{1,7},{3,1},{5,3},{7,5},{8,14},{10,8},{12,... | collective-permute-start | bytes 5505032 | tf_op jit(solution)/shard_map/ppermute | solution.py:333
  349.9 86.2 %collective-permute-start.7 = (bf16[512,2,896]{2,1,0:T(2,128)(2,1)}, bf16[512,2,896]{2,1,0:T(2,128)(2,1)}, u32[]{:S(2)}, u32[]{:S(2)}) collective-permute-start(bf16[512,2,896]{2,1,0:T(2,128)(2,1)} %reshape.160), channel_id=1, source_target_pairs={{0,4},{2,6},{4,0},{6,2},{1,5},{3,7},{5,1},{7,3},{8,12},{10,14},{12... | collective-permute-start | bytes 5505032 | tf_op jit(solution)/shard_map/ppermute | solution.py:333
  363.2 72.9 %collective-permute-start.6 = (bf16[512,2,896]{2,1,0:T(2,128)(2,1)}, bf16[512,2,896]{2,1,0:T(2,128)(2,1)}, u32[]{:S(2)}, u32[]{:S(2)}) collective-permute-start(bf16[512,2,896]{2,1,0:T(2,128)(2,1)} %reshape.159), channel_id=1, source_target_pairs={{0,2},{2,4},{4,6},{6,0},{1,3},{3,5},{5,7},{7,1},{8,10},{10,12},{12... | collective-permute-start | bytes 5505032 | tf_op jit(solution)/shard_map/ppermute | solution.py:333
Sparse Core Ops, SparseCore 0:
  11.0 37.2 all-gather.7
  50.4 27.0 all-gather.5
  79.3 122.7 all-gather.9

commit v3 on v2

--- a/solution.py
+++ b/solution.py
@@ -329,7 +329,7 @@
             preferred_element_type=jnp.float32,
         )
         squares = squares + jnp.sum(block * block)
-        sent = block.astype(jnp.bfloat16).reshape(block_width, 2, units)
+        sent = block.astype(jnp.bfloat16)
         received[k] = lax.ppermute(sent, "dp", shifted_perm(k)) if k else sent
     squares = sum_everywhere(squares)
     scale = lax.rsqrt(squares / (2 * D * FF) + 1e-06)
@@ -339,7 +339,7 @@
         for j in range(chips)
     ]
     weight_step = jnp.concatenate(
-        pieces, axis=2
+        [piece.reshape(block_width, 2, units) for piece in pieces], axis=2
     )
     weight_step = (weight_step.astype(jnp.float32) * scale).astype(jnp.bfloat16)
     column_count = width // lax.axis_size("tensor")

time: 500 us -> 468 us (0.936)
  other arithmetic: 65.3 us -> 34.2 us
  Pallas kernels: 195 us -> 202 us
    convert_element_type x1, other arithmetic: 33.5 us -> 13.7 us  [per_device(): weight_step = (weight_step.astype(jnp.float32) * scale).astype(jnp.bfloat16)]
    another operation x1, other arithmetic: 14.9 us -> 3.59 us  [per_device(): stacked = jnp.stack(received)]
    pallas_call x1, Pallas kernels: 53.7 us -> 61.1 us  [sum_everywhere(): pl.pallas_call(functools.partial(scalar_kernel, tensors, chips, cores), o...]
    squeeze x2 -> x1, local copies, waits for them, and re-layouts: 6.39 us -> 1.27 us  [per_device(): lax.dynamic_index_in_dim(stacked, lax.rem(chip - j + chips, chips), 0, ke...]
    reshape x3 -> x4, local copies, waits for them, and re-layouts: 13.9 us -> 15.4 us  [per_device(): piece.reshape(block_width, 2, units)]
  transfers between devices with their start and end apart: 12 -> 12, of which waited for: 2 -> 2; matrix products, arithmetic and copies ran while one was open for 27% -> 25% of each run, Pallas kernels for 34% -> 38%
where the time goes in v3:
time: 468 us; the launch traced here: 464 us
  Pallas kernels  202 us (43%)
  matrix products  111 us (24%)
  waiting for transfers between devices  51.2 us (11%)
  local copies, waits for them, and re-layouts  38.1 us (8%)
  other arithmetic  34.2 us (7%)
  between operations  19.2 us (4%)
  starting transfers between devices  8.68 us (2%)
    pallas_call x3, Pallas kernels, apply_step(): pl.pallas_call(functools.partial(step_kernel, tensors, chips, cores), out...  120 us
    pallas_call x1, Pallas kernels, sum_everywhere(): pl.pallas_call(functools.partial(scalar_kernel, tensors, chips, cores), o...  61.1 us
    dot_general x4, matrix products, hidden_grads(): jnp.dot(normalized, weight_pair, preferred_element_type=jnp.float32)  35.8 us
    dot_general x3, matrix products, per_device(): lax.dot_general(unit_grads, weight_pair, (((1,), (1,)), ((), ())), prefer...  32.3 us
    all_gather x1, waiting for transfers between devices, per_device(): lax.all_gather(unit_slice.reshape(half, 2 * units), 'replica', axis=0, ti...  27.4 us
    dot_general x4, matrix products, per_device(): lax.dot_general(lax.dynamic_slice_in_dim(other_normed, start, block_width...  26.3 us
    all_gather x1, waiting for transfers between devices, per_device(): package = lax.all_gather(package, 'dp', axis=0, tiled=False)  23.7 us
    pallas_call x2, Pallas kernels, normed_rows(): pl.pallas_call(norm_kernel, out_shape=jax.ShapeDtypeStruct(states.shape,...  20.4 us
  transfers between devices with their start and end apart: 12, of which 2 were waited for; matrix products, arithmetic and copies ran while one was open for 25% of the time, Pallas kernels for 38%

profile of v3, /device:TPU:0, one launch (start us, length us, event | category | flops | bytes accessed | tf_op | source)
XLA Modules:
  0.0 464.2 jit_solution(3592999053239750435)
XLA Ops:
  7.9 1.0 dynamic-slice_bitcast_fusion.6
  8.9 1.0 dynamic-slice_bitcast_fusion.5
  9.9 0.9 maximum_maximum_fusion
  10.9 6.5 %constant_dynamic-slice_fusion.9 = bf16[2048,2,896]{2,1,0:T(2,128)(2,1)S(1)} fusion(bf16[2048,2,3584]{2,1,0:T(2,128)(2,1)} %param.10, s32[]{:T(128)S(6)} %select_n.64), kind=kLoop, calls=%fused_computation.130 | loop fusion | bytes 14680068 | tf_op jit(solution)/shard_map/dynamic_slice | solution.py:243
  17.4 4.6 copy.14
  24.6 23.7 %all-gather.8.cloned.1.call-done = bf16[128,7808]{1,0:T(8,128)(2,1)} async-done(((bf16[32,7808]{1,0:T(8,128)(2,1)}), bf16[128,7808]{1,0:T(8,128)(2,1)}) %all-gather.8.cloned.1.call-update) | async-done | bytes 1998864 | tf_op jit(solution)/shard_map/all_gather | solution.py:257
  48.2 1.7 fusion.29
  50.0 27.4 %all-gather.6.cloned.1.call-done = bf16[4096,1792]{1,0:T(8,128)(2,1)} async-done(((bf16[2048,1792]{1,0:T(8,128)(2,1)}), bf16[4096,1792]{1,0:T(8,128)(2,1)}) %all-gather.6.cloned.1.call-update) | async-done | bytes 14680080 | tf_op jit(solution)/shard_map/all_gather | solution.py:244
  78.1 7.3 %fusion.85 = f32[128,1792]{1,0:T(8,128)S(1)} fusion(bf16[128,4096]{1,0:T(8,128)(2,1)S(1)} %bitcast.136, bf16[4096,1792]{1,0:T(8,128)(2,1)} %all-gather.6.cloned.1.call-done), kind=kOutput, calls=%fused_computation.147 | convolution fusion | flops 1879048192 | bytes 16646144 | tf_op jit(solution)/shard_map/dot_general | solution.py:29
  85.6 12.1 %fusion.58 = f32[128,4096]{1,0:T(8,128)S(1)} fusion(bf16[4096,1792]{1,0:T(8,128)(2,1)} %all-gather.6.cloned.1.call-done, bf16[128,896]{1,0:T(8,128)(2,1)S(1)} %get-tuple-element.37, bf16[128,896]{1,0:T(8,128)(2,1)S(1)} %get-tuple-element.36), kind=kOutput, calls=%fused_computation.91 | convolution fusion | flops 1879965696 | bytes 17235968 | tf_op jit(solution)/shard_map/dot_general | solution.py:295
  98.3 0.7 fusion.34
  99.3 33.3 %attack_step.3.adversary_ref = f32[32,8,512]{2,1,0:T(8,128)S(1)} custom-call(f32[32,8,512]{2,1,0:T(8,128)S(1)} %bitcast.91, f32[32,8,512]{2,1,0:T(8,128)S(1)} %bitcast.86, f32[1]{0:T(128)} %get-tuple-element.48.step_ref), custom_call_target="tpu_custom_call" | custom-call | flops 20000000000 | bytes 1572864 | tf_op jit(solution)/shard_map/attack_step/pallas_call | solution.py:110
  133.7 2.1 fusion.86
  136.1 10.2 %fusion.62 = f32[128,4096]{1,0:T(8,128)S(1)} fusion(bf16[4096,1792]{1,0:T(8,128)(2,1)} %all-gather.6.cloned.1.call-done, bf16[128,896]{1,0:T(8,128)(2,1)S(1)} %get-tuple-element.35, bf16[128,896]{1,0:T(8,128)(2,1)S(1)} %get-tuple-element.34), kind=kOutput, calls=%fused_computation.95 | convolution fusion | flops 1879965696 | bytes 17235968 | tf_op jit(solution)/shard_map/dot_general | solution.py:295
  146.9 0.7 fusion.27
  148.8 1.9 collective-permute-start.2
  150.6 1.7 collective-permute-start.1
  152.3 63.3 %attack_step.4 = f32[32,8,512]{2,1,0:T(8,128)S(1)} custom-call(f32[32,8,512]{2,1,0:T(8,128)S(1)} %bitcast.88, f32[32,8,512]{2,1,0:T(8,128)S(1)} %attack_step.3.adversary_ref, f32[1]{0:T(128)} %get-tuple-element.49.step_ref), custom_call_target="tpu_custom_call" | custom-call | flops 20000000000 | bytes 1572864 | tf_op jit(solution)/shard_map/attack_step/pallas_call | solution.py:110
  216.3 1.3 dynamic-slice_bitcast_fusion.3
  218.3 7.3 %fusion.87 = f32[128,1792]{1,0:T(8,128)S(1)} fusion(bf16[128,4096]{1,0:T(8,128)(2,1)S(1)} %bitcast.138, bf16[4096,1792]{1,0:T(8,128)(2,1)} %all-gather.6.cloned.1.call-done), kind=kOutput, calls=%fused_computation.149 | convolution fusion | flops 1879048192 | bytes 16646144 | tf_op jit(solution)/shard_map/dot_general | solution.py:29
  225.8 10.0 %fusion.66 = f32[128,4096]{1,0:T(8,128)S(1)} fusion(bf16[4096,1792]{1,0:T(8,128)(2,1)} %all-gather.6.cloned.1.call-done, bf16[128,896]{1,0:T(8,128)(2,1)S(1)} %get-tuple-element.33, bf16[128,896]{1,0:T(8,128)(2,1)S(1)} %get-tuple-element.32), kind=kOutput, calls=%fused_computation.99 | convolution fusion | flops 1879965696 | bytes 17235968 | tf_op jit(solution)/shard_map/dot_general | solution.py:295
  236.4 0.7 fusion.20
  237.7 23.8 %attack_step.5 = f32[32,8,512]{2,1,0:T(8,128)S(1)} custom-call(f32[32,8,512]{2,1,0:T(8,128)S(1)} %bitcast.89, f32[32,8,512]{2,1,0:T(8,128)S(1)} %bitcast.90, f32[1]{0:T(128)} %get-tuple-element.47.step_ref), custom_call_target="tpu_custom_call" | custom-call | flops 20000000000 | bytes 1572864 | tf_op jit(solution)/shard_map/attack_step/pallas_call | solution.py:110
  262.0 0.7 collective-permute-start.4
  262.8 10.4 %normed_rows.2 = bf16[4,256,4096]{2,1,0:T(8,128)(2,1)} custom-call(s32[4]{0:T(128)S(1)} %fusion.78.start_ref, bf16[4,256,4096]{2,1,0:T(8,128)(2,1)} %bitcast.7.state_ref, bf16[96,4096]{1,0:T(8,128)(2,1)S(1)} %pad_maximum_fusion.4.parts_ref, f32[1,4096]{1,0:T(1,128)S(1)} %bitcast.84), custom_call_target="tpu_custom_call" | custom-call | flops 838860800 | bytes 16777216 | tf_op jit(solution)/shard_map/normed_rows/pallas_call | solution.py:212
  273.2 19.2 %fusion.88 = f32[1024,1792]{1,0:T(8,128)S(1)} fusion(bf16[1024,4096]{1,0:T(8,128)(2,1)} %bitcast.131, bf16[4096,1792]{1,0:T(8,128)(2,1)} %all-gather.6.cloned.1.call-done), kind=kOutput, calls=%fused_computation.150 | convolution fusion | flops 15032385536 | bytes 30408704 | tf_op jit(solution)/shard_map/dot_general | solution.py:29
  292.4 4.8 %fusion.1 = (bf16[1024,896]{1,0:T(8,128)(2,1)S(1)}, bf16[1024,896]{1,0:T(8,128)(2,1)S(1)}) fusion(f32[1024,1792]{1,0:T(8,128)S(1)} %fusion.88, bf16[256,896]{1,0:T(8,128)(2,1)S(1)} %copy-done.6, bf16[256,896]{1,0:T(8,128)(2,1)S(1)} %copy-done.7, bf16[256,896]{1,0:T(8,128)(2,1)S(1)} %copy-done.8, bf16[256,896]{1,0:T(8,128)(2,1)S(1)} %copy-done.5), kind=kLoop, calls=%fused_computation.5 | loop fusion | flops 19267584 | bytes 12845056 | tf_op jit(solution)/shard_map/convert.2
  297.2 2.3 pad_maximum_fusion.1
  300.1 4.1 fusion.37
  304.2 3.4 fusion.40
  307.6 3.4 fusion.43
  311.0 10.0 %normed_rows.3 = bf16[4,256,4096]{2,1,0:T(8,128)(2,1)} custom-call(s32[4]{0:T(128)S(1)} %collective-permute-done.3.start_ref, bf16[4,256,4096]{2,1,0:T(8,128)(2,1)} %collective-permute-done.4.state_ref, bf16[96,4096]{1,0:T(8,128)(2,1)S(1)} %pad_maximum_fusion.4.parts_ref, f32[1,4096]{1,0:T(1,128)S(1)} %bitcast.85), custom_call_target="tpu_custom_call" | custom-call | flops 838860800 | bytes 16777216 | tf_op jit(solution)/shard_map/normed_rows/pallas_call | solution.py:212
  321.0 6.6 %multiply_reduce_fusion.1 = (f32[]{:T(128)}, bf16[512,1792]{1,0:T(8,128)(2,1)}) fusion(f32[512,1792]{1,0:T(8,128)S(1)} %fusion.37, bf16[1024,1792]{1,0:T(8,128)(2,1)} %collective-permute-done.5, bf16[1024,4096]{1,0:T(8,128)(2,1)} %bitcast.123, s32[]{:T(128)S(6)} %select_n.79), kind=kOutput, calls=%fused_computation.9 | convolution fusion | flops 1882718208 | bytes 10223624 | tf_op jit(solution)/shard_map/dot_general | solution.py:327
  327.5 2.0 collective-permute-start.8
  329.5 6.5 %multiply_reduce_fusion.3 = (f32[]{:T(128)}, bf16[512,1792]{1,0:T(8,128)(2,1)}) fusion(f32[512,1792]{1,0:T(8,128)S(1)} %fusion.40, bf16[1024,1792]{1,0:T(8,128)(2,1)} %collective-permute-done.5, bf16[1024,4096]{1,0:T(8,128)(2,1)} %bitcast.124, s32[]{:T(128)S(6)} %select_n.78), kind=kOutput, calls=%fused_computation.11 | convolution fusion | flops 1882718208 | bytes 10223624 | tf_op jit(solution)/shard_map/dot_general | solution.py:327
  336.0 1.1 collective-permute-start.7
  337.1 6.5 %multiply_reduce_fusion.2 = (f32[]{:T(128)}, bf16[512,1792]{1,0:T(8,128)(2,1)}) fusion(f32[512,1792]{1,0:T(8,128)S(1)} %fusion.43, bf16[1024,1792]{1,0:T(8,128)(2,1)} %collective-permute-done.5, bf16[1024,4096]{1,0:T(8,128)(2,1)} %bitcast.125, s32[]{:T(128)S(6)} %select_n.77), kind=kOutput, calls=%fused_computation.10 | convolution fusion | flops 1882718208 | bytes 10223624 | tf_op jit(solution)/shard_map/dot_general | solution.py:327
  344.1 0.7 constant_dynamic-slice_fusion.7
  344.8 5.8 %fusion.46 = f32[512,1792]{1,0:T(8,128)} fusion(bf16[1024,4096]{1,0:T(8,128)(2,1)} %bitcast.135, s32[]{:T(128)S(6)} %select_n.67, bf16[1024,896]{1,0:T(8,128)(2,1)} %copy-done.2, bf16[1024,896]{1,0:T(8,128)(2,1)S(1)} %get-tuple-element.10), kind=kOutput, calls=%fused_computation.67 | convolution fusion | flops 1886388224 | bytes 8388612 | tf_op jit(solution)/shard_map/dot_general | solution.py:324
  352.6 6.7 %multiply_reduce_fusion = (f32[]{:T(128)}, bf16[1,512,1792]{2,1,0:T(8,128)(2,1)S(1)}) fusion(f32[512,1792]{1,0:T(8,128)} %fusion.46, bf16[1024,1792]{1,0:T(8,128)(2,1)} %collective-permute-done.5, bf16[1024,4096]{1,0:T(8,128)(2,1)} %bitcast.126, s32[]{:T(128)S(6)} %select_n.67), kind=kOutput, calls=%fused_computation.8 | convolution fusion | flops 1882718208 | bytes 10223624 | tf_op jit(solution)/shard_map/dot_general | solution.py:327
  359.9 61.1 %scalar_sum.1 = f32[8,128]{1,0:T(8,128)S(1)} custom-call(f32[8,128]{1,0:T(8,128)S(1)} %broadcast_in_dim.20.value_ref), custom_call_target="tpu_custom_call" | custom-call | tf_op jit(solution)/shard_map/scalar_sum/pallas_call | solution.py:177
  422.2 3.6 pad_maximum_fusion
  425.8 2.6 constant_dynamic-slice_fusion.3
  428.4 4.6 reshape.169
  433.0 4.6 reshape.168
  437.7 4.6 %reshape.167 = bf16[512,2,896]{2,1,0:T(2,128)(2,1)} reshape(bf16[1,512,1792]{2,1,0:T(8,128)(2,1)} %get-tuple-element.15) | data formatting | bytes 3670016 | tf_op jit(solution)/shard_map/reshape | solution.py:342
  442.3 1.5 reshape.166
  443.8 13.7 %multiply_convert_fusion = bf16[512,2,3584]{2,1,0:T(2,128)(2,1)} fusion(bf16[512,2,896]{2,1,0:T(2,128)(2,1)} %reshape.169, bf16[512,2,896]{2,1,0:T(2,128)(2,1)} %reshape.168, bf16[512,2,896]{2,1,0:T(2,128)(2,1)} %reshape.167, bf16[512,2,896]{2,1,0:T(2,128)(2,1)} %reshape.166, f32[]{:T(128)} %bitcast.32), kind=kLoop, calls=%fused_computation | loop fusion | flops 36700160 | bytes 14680068 | tf_op jit(solution)/shard_map/convert_element_type | solution.py:344
  (90 shorter events, 11.7 us)
Async XLA Ops:
  7.2 41.1 %all-gather.8.cloned.1.call-start = ((), (), s32[]{:S(2)}) async-start(), calls=%async_computation.1 | async-start | bytes 2498560 | tf_op jit(solution)/shard_map/all_gather | solution.py:257
  10.8 66.6 %all-gather.6.cloned.1.call-start = ((), (), s32[]{:S(2)}) async-start(), calls=%async_computation | async-start | bytes 22020096 | tf_op jit(solution)/shard_map/all_gather | solution.py:244
  21.9 1.0 copy-start.9
  21.9 2.0 copy-start.10
  22.0 195.6 %all-gather.10.cloned.1.call-start = ((), (), s32[]{:S(2)}) async-start(), calls=%async_computation.2 | async-start | bytes 10485760 | tf_op jit(solution)/shard_map/all_gather | solution.py:268
  23.2 54.2 %copy-start = (f32[4096]{0:T(1024)S(1)}, f32[4096]{0:T(1024)}, u32[]{:S(2)}) copy-start(f32[4096]{0:T(1024)} %param.9) | copy-start | bytes 49156
  48.2 29.2 %copy-start.1 = (bf16[128,7808]{1,0:T(8,128)(2,1)S(1)}, bf16[128,7808]{1,0:T(8,128)(2,1)}, u32[]{:S(2)}) copy-start(bf16[128,7808]{1,0:T(8,128)(2,1)} %all-gather.8.cloned.1.call-done) | copy-start | bytes 5996548
  98.3 35.4 %slice-start = ((s8[14680064]{0:T(1024)(128)(4,1)}), s8[4194304]{0:T(1024)(128)(4,1)S(1)}, s32[]{:S(2)}) async-start(s8[14680064]{0:T(1024)(128)(4,1)} %bitcast.94), calls=%async_computation.3 | async-start | bytes 8388608
  99.3 34.4 %slice-start.1 = ((s8[14680064]{0:T(1024)(128)(4,1)}), s8[4194304]{0:T(1024)(128)(4,1)S(1)}, s32[]{:S(2)}) async-start(s8[14680064]{0:T(1024)(128)(4,1)} %bitcast.94), calls=%async_computation.4 | async-start | bytes 8388608
  99.3 34.4 %slice-start.2 = ((s8[14680064]{0:T(1024)(128)(4,1)}), s8[4194304]{0:T(1024)(128)(4,1)S(1)}, s32[]{:S(2)}) async-start(s8[14680064]{0:T(1024)(128)(4,1)} %bitcast.94), calls=%async_computation.5 | async-start | bytes 8388608
  99.3 34.4 %slice-start.3 = ((s8[14680064]{0:T(1024)(128)(4,1)}), s8[2097152]{0:T(1024)(128)(4,1)S(1)}, s32[]{:S(2)}) async-start(s8[14680064]{0:T(1024)(128)(4,1)} %bitcast.94), calls=%async_computation.6 | async-start | bytes 4194304
  146.9 1.5 copy-start.4
  148.8 67.2 %collective-permute-start.2 = (bf16[256,896]{1,0:T(8,128)(2,1)S(1)}, bf16[256,896]{1,0:T(8,128)(2,1)S(1)}, u32[]{:S(2)}, u32[]{:S(2)}) collective-permute-start(bf16[256,896]{1,0:T(8,128)(2,1)S(1)} %get-tuple-element.29), channel_id=1, source_target_pairs={{0,6},{2,0},{4,2},{6,4},{1,7},{3,1},{5,3},{7,5},{8,14},{10,8},{12,... | collective-permute-start | bytes 1376264 | tf_op jit(solution)/shard_map/ppermute | solution.py:279
  150.6 65.4 %collective-permute-start.1 = (bf16[256,896]{1,0:T(8,128)(2,1)S(1)}, bf16[256,896]{1,0:T(8,128)(2,1)S(1)}, u32[]{:S(2)}, u32[]{:S(2)}) collective-permute-start(bf16[256,896]{1,0:T(8,128)(2,1)S(1)} %get-tuple-element.30), channel_id=1, source_target_pairs={{0,4},{2,6},{4,0},{6,2},{1,5},{3,7},{5,1},{7,3},{8,12},{10,14},{12... | collective-permute-start | bytes 1376264 | tf_op jit(solution)/shard_map/ppermute | solution.py:279
  152.3 63.7 %collective-permute-start = (bf16[256,896]{1,0:T(8,128)(2,1)S(1)}, bf16[256,896]{1,0:T(8,128)(2,1)S(1)}, u32[]{:S(2)}, u32[]{:S(2)}) collective-permute-start(bf16[256,896]{1,0:T(8,128)(2,1)S(1)} %get-tuple-element.31), channel_id=1, source_target_pairs={{0,2},{2,4},{4,6},{6,0},{1,3},{3,5},{5,7},{7,1},{8,10},{10,12},{12... | collective-permute-start | bytes 1376264 | tf_op jit(solution)/shard_map/ppermute | solution.py:279
  262.0 49.0 %collective-permute-start.4 = (bf16[4,256,4096]{2,1,0:T(8,128)(2,1)}, bf16[4,256,4096]{2,1,0:T(8,128)(2,1)}, u32[]{:S(2)}, u32[]{:S(2)}) collective-permute-start(bf16[4,256,4096]{2,1,0:T(8,128)(2,1)} %bitcast.7.state_ref), channel_id=1, source_target_pairs={{0,1},{1,0},{2,3},{3,2},{4,5},{5,4},{6,7},{7,6},{8,9},{9,8},{10,11... | collective-permute-start | bytes 25165832 | tf_op jit(solution)/shard_map/ppermute | solution.py:307
  273.1 19.2 %copy-start.5 = (bf16[256,896]{1,0:T(8,128)(2,1)S(1)}, bf16[256,896]{1,0:T(8,128)(2,1)}, u32[]{:S(2)}) copy-start(bf16[256,896]{1,0:T(8,128)(2,1)} %get-tuple-element.24) | copy-start | bytes 1376260
  273.1 19.2 %copy-start.6 = (bf16[256,896]{1,0:T(8,128)(2,1)S(1)}, bf16[256,896]{1,0:T(8,128)(2,1)}, u32[]{:S(2)}) copy-start(bf16[256,896]{1,0:T(8,128)(2,1)} %get-tuple-element.25) | copy-start | bytes 1376260
  273.2 19.2 %copy-start.7 = (bf16[256,896]{1,0:T(8,128)(2,1)S(1)}, bf16[256,896]{1,0:T(8,128)(2,1)}, u32[]{:S(2)}) copy-start(bf16[256,896]{1,0:T(8,128)(2,1)} %get-tuple-element.26) | copy-start | bytes 1376260
  273.2 19.2 %copy-start.8 = (bf16[256,896]{1,0:T(8,128)(2,1)S(1)}, bf16[256,896]{1,0:T(8,128)(2,1)}, u32[]{:S(2)}) copy-start(bf16[256,896]{1,0:T(8,128)(2,1)} %get-tuple-element.27) | copy-start | bytes 1376260
  297.2 2.4 copy-start.2
  299.6 21.4 %collective-permute-start.5 = (bf16[1024,1792]{1,0:T(8,128)(2,1)}, bf16[1024,1792]{1,0:T(8,128)(2,1)}, u32[]{:S(2)}, u32[]{:S(2)}) collective-permute-start(bf16[1024,1792]{1,0:T(8,128)(2,1)} %pad_maximum_fusion.1), channel_id=1, source_target_pairs={{0,1},{1,0},{2,3},{3,2},{4,5},{5,4},{6,7},{7,6},{8,9},{9,8},{10,11... | collective-permute-start | bytes 11010056 | tf_op jit(solution)/shard_map/ppermute | solution.py:315
  299.6 4.6 copy-start.3
  299.6 11.3 %collective-permute-start.3 = (s32[4]{0:T(128)S(1)}, s32[4]{0:T(128)S(1)}, u32[]{:S(2)}, u32[]{:S(2)}) collective-permute-start(s32[4]{0:T(128)S(1)} %fusion.78.start_ref), channel_id=1, source_target_pairs={{0,1},{1,0},{2,3},{3,2},{4,5},{5,4},{6,7},{7,6},{8,9},{9,8},{10,11... | collective-permute-start | bytes 56 | tf_op jit(solution)/shard_map/ppermute | solution.py:269
  327.5 94.7 %collective-permute-start.8 = (bf16[512,1792]{1,0:T(8,128)(2,1)}, bf16[512,1792]{1,0:T(8,128)(2,1)}, u32[]{:S(2)}, u32[]{:S(2)}) collective-permute-start(bf16[512,1792]{1,0:T(8,128)(2,1)} %get-tuple-element.19), channel_id=1, source_target_pairs={{0,6},{2,0},{4,2},{6,4},{1,7},{3,1},{5,3},{7,5},{8,14},{10,8},{12,... | collective-permute-start | bytes 5505032 | tf_op jit(solution)/shard_map/ppermute | solution.py:333
  336.0 86.2 %collective-permute-start.7 = (bf16[512,1792]{1,0:T(8,128)(2,1)}, bf16[512,1792]{1,0:T(8,128)(2,1)}, u32[]{:S(2)}, u32[]{:S(2)}) collective-permute-start(bf16[512,1792]{1,0:T(8,128)(2,1)} %get-tuple-element.23), channel_id=1, source_target_pairs={{0,4},{2,6},{4,0},{6,2},{1,5},{3,7},{5,1},{7,3},{8,12},{10,14},{12... | collective-permute-start | bytes 5505032 | tf_op jit(solution)/shard_map/ppermute | solution.py:333
  343.7 78.5 %collective-permute-start.6 = (bf16[512,1792]{1,0:T(8,128)(2,1)}, bf16[512,1792]{1,0:T(8,128)(2,1)}, u32[]{:S(2)}, u32[]{:S(2)}) collective-permute-start(bf16[512,1792]{1,0:T(8,128)(2,1)} %get-tuple-element.21), channel_id=1, source_target_pairs={{0,2},{2,4},{4,6},{6,0},{1,3},{3,5},{5,7},{7,1},{8,10},{10,12},{12... | collective-permute-start | bytes 5505032 | tf_op jit(solution)/shard_map/ppermute | solution.py:333
Sparse Core Ops, SparseCore 0:
  11.0 37.2 all-gather.7
  50.4 27.0 all-gather.5
  79.3 122.7 all-gather.9
